TPU v7x, 256 devices: a whole 4x4x8 slice. The times are simulated.
256 devices in a mesh: req: 16 (over y_lo, z), tensor: 16 (over y_hi, x, core).
Axes of the slice: x: 4, y: 4 (y_hi: 2, y_lo: 2; y = y_hi * 2 + y_lo), z: 8, core: 2. Of those that a mesh axis runs over, the one named last changes fastest.
Arguments:
- activations: bfloat16 [8192, 8192], P(('req', 'tensor')), parts along dimension 0, may hold values from -6 to 6
- norm_gain: float32 [8192], replicated, may hold values from 0.1 to 1.9
- query_weight: bfloat16 [8192, 4096], P(None, 'tensor'), may hold values from -0.0625 to 0.0625
- keyvalue_weight: bfloat16 [8192, 2048], P(None, 'tensor'), may hold values from -0.0625 to 0.0625
- output_weight: bfloat16 [4096, 8192], P('tensor'), may hold values from -0.09375 to 0.09375
- page_pool: bfloat16 [2048, 128, 256], P(('req', 'tensor')), parts along dimension 0, may hold values from -320 to 320
- page_table: int32 [288, 8], P('req'), parts along dimension 0, may hold values from 0 to 15
- prefill_offsets: int32 [32], P('req'), parts along dimension 0, may hold values from 0 to 1024, as said below
- decode_lengths: int32 [256], P('req'), parts along dimension 0, may hold values from 1 to 1024, as said below
Outputs:
- block_output: bfloat16 [8192, 8192], P(('req', 'tensor')), parts along dimension 0
There are 16 independent parts, one for each index of `req`. A program takes and returns all parts, laid end to end along the dimension named above; an argument that names none is the same for every part. Nothing has to cross between parts.
Inputs may be any that keep to these rules, and one draw needn't show every extreme that they name: `page_table`: pages may be shared between requests. `decode_lengths`: some decode request has exactly 1024 cached tokens. `prefill_offsets`: some stretch has exactly 1024 cached tokens before it.
All inputs are finite; a program needn't handle non-finite values.
Results may differ from a plain program's by a relative error of at most 0.0095.
The roundings to bfloat16 on the way count: a program that leaves them out, or rounds other values in their place, can miss the bound.
Values may be sent and summed in bfloat16 or wider, within the bound.
A program may use at most 128 MiB of HBM per device.

v0:
```python
import jax
import jax.numpy as jnp
from jax import lax
from jax.sharding import PartitionSpec as P

QH = 32
KVH = 8
HD = 128
C = 248


eps_norm = 1e-06
rope_base = 1000000.0
neg_big = -1e30


def partner(array, axis, distance):
    return lax.ppermute(array, axis, [(i, i ^ 1 << distance) for i in range(lax.axis_size(axis))])


def rotate(values, positions):
    half_dim = values.shape[-1] // 2
    frequency = rope_base ** (-2.0 * jnp.arange(half_dim, dtype=jnp.float32) / values.shape[-1])
    angles = positions.astype(jnp.float32)[:, None] * frequency[None, :]
    cosine = jnp.cos(angles)[:, None, :]
    sine_part = jnp.sin(angles)[:, None, :]
    first_half = values[..., :half_dim]
    second_half = values[..., half_dim:]
    return jnp.concatenate(
        [
            first_half * cosine - second_half * sine_part,
            second_half * cosine + first_half * sine_part,
        ],
        axis=-1,
    )


def cached_block(queries, table_row, key_limit, pool_rows, page_lo):
    held_pages = pool_rows.shape[1]
    page_len = pool_rows.shape[2]
    head_dim = queries.shape[-1]
    local_page = table_row - page_lo
    owned_page = (local_page >= 0) & (local_page < held_pages)
    local_page = jnp.clip(local_page, 0, held_pages - 1)
    fetched = jnp.take(pool_rows, local_page, axis=1)
    key_span = fetched.shape[1] * page_len
    key_rows = fetched.reshape(pool_rows.shape[0], key_span, 2 * head_dim)
    slot_ids = jnp.arange(key_span, dtype=jnp.int32)
    visible = jnp.repeat(owned_page, page_len, total_repeat_length=key_span) & (
        slot_ids < key_limit
    )
    scores = jnp.einsum(
        "rkgd,ksd->kgrs", queries, key_rows[:, :, :head_dim], preferred_element_type=jnp.float32
    ) * head_dim ** (-0.5)
    scores = jnp.where(visible, scores, neg_big)
    highest = jnp.max(scores, axis=-1)
    weights = jnp.where(visible, jnp.exp(scores - highest[..., None]), 0.0)
    totals = jnp.sum(weights, axis=-1)
    blended = jnp.einsum(
        "kgrs,ksd->rkgd",
        weights.astype(jnp.bfloat16),
        key_rows[:, :, head_dim:],
        preferred_element_type=jnp.float32,
    )
    return (jnp.transpose(highest, (2, 0, 1)), jnp.transpose(totals, (2, 0, 1)), blended)


def cached_all(
    queries, pool_rows, page_lo, page_table, prefill_offsets, decode_lengths, stretch_len
):
    pieces = []
    for stretch_id in range(2):
        lower = stretch_id * stretch_len
        pieces.append(
            cached_block(
                queries[lower : lower + stretch_len],
                page_table[stretch_id],
                prefill_offsets[stretch_id],
                pool_rows,
                page_lo,
            )
        )

    def decode_one(decode_item):
        query_row, table_row, length_one = decode_item
        return cached_block(query_row[None], table_row, length_one, pool_rows, page_lo)

    decoded = lax.map(decode_one, (queries[2 * stretch_len :], page_table[2:], decode_lengths))
    decoded = tuple((stacked[:, 0] for stacked in decoded))
    return tuple(
        (
            jnp.concatenate([pieces[0][part_id], pieces[1][part_id], decoded[part_id]], axis=0)
            for part_id in range(3)
        )
    )


def stretch_self(queries, new_keys, new_values):
    length_q = queries.shape[0]
    scores = jnp.einsum(
        "rkgd,skd->kgrs", queries, new_keys, preferred_element_type=jnp.float32
    ) * queries.shape[-1] ** (-0.5)
    counter = jnp.arange(length_q, dtype=jnp.int32)
    causal = counter[:, None] >= counter[None, :]
    scores = jnp.where(causal, scores, neg_big)
    highest = jnp.max(scores, axis=-1)
    weights = jnp.where(causal, jnp.exp(scores - highest[..., None]), 0.0)
    totals = jnp.sum(weights, axis=-1)
    blended = jnp.einsum(
        "kgrs,skd->rkgd",
        weights.astype(jnp.bfloat16),
        new_values,
        preferred_element_type=jnp.float32,
    )
    return (jnp.transpose(highest, (2, 0, 1)), jnp.transpose(totals, (2, 0, 1)), blended)


def fresh_all(queries, new_keys, new_values, stretch_len):
    pieces = []
    for stretch_id in range(2):
        lower = stretch_id * stretch_len
        upper = lower + stretch_len
        pieces.append(
            stretch_self(queries[lower:upper], new_keys[lower:upper], new_values[lower:upper])
        )
    tail_q = queries[2 * stretch_len :]
    own_score = jnp.einsum(
        "rkgd,rkd->rkg", tail_q, new_keys[2 * stretch_len :], preferred_element_type=jnp.float32
    ) * queries.shape[-1] ** (-0.5)
    own_values = jnp.broadcast_to(
        new_values[2 * stretch_len :].astype(jnp.float32)[:, :, None, :], tail_q.shape
    )
    decoded = (own_score, jnp.ones_like(own_score), own_values)
    return tuple(
        (
            jnp.concatenate([pieces[0][part_id], pieces[1][part_id], decoded[part_id]], axis=0)
            for part_id in range(3)
        )
    )


def combine_parts(first, second):
    highest = jnp.maximum(first[0], second[0])
    first_scale = jnp.exp(first[0] - highest)
    second_scale = jnp.exp(second[0] - highest)
    totals = first_scale * first[1] + second_scale * second[1]
    blended = first_scale[..., None] * first[2] + second_scale[..., None] * second[2]
    return (highest, totals, blended)


def shards(
    activations,
    norm_gain,
    query_weight,
    keyvalue_weight,
    output_weight,
    page_pool,
    page_table,
    prefill_offsets,
    decode_lengths,
):
    my_index = lax.axis_index("tensor")
    parity = my_index % 2
    local_q = query_weight.shape[1] // HD
    group = QH // KVH
    widened = activations.astype(jnp.float32)
    normed = (
        widened
        * lax.rsqrt(jnp.mean(widened * widened, axis=-1, keepdims=True) + eps_norm)
        * norm_gain
    ).astype(jnp.bfloat16)
    project_piece = lax.all_gather(normed, "tensor", axis=0, tiled=True)
    joint = jnp.concatenate(
        [
            jnp.dot(project_piece, query_weight, preferred_element_type=jnp.float32),
            jnp.dot(project_piece, keyvalue_weight, preferred_element_type=jnp.float32),
        ],
        axis=1,
    )
    row_count = joint.shape[0]
    inner = jnp.arange(C, dtype=jnp.int32)
    positions = jnp.concatenate(
        [prefill_offsets[0] + inner, prefill_offsets[1] + inner, decode_lengths]
    )
    own_q = rotate(joint[:, : local_q * HD].reshape(row_count, local_q, HD), positions).astype(
        jnp.bfloat16
    )
    kv_cols = joint[:, local_q * HD :]
    kv_local = 1
    turned = rotate(kv_cols[:, None, :], positions)[:, 0, :]
    own_half = jnp.where(parity == 0, turned, kv_cols).astype(jnp.bfloat16)
    other_half = partner(own_half, "tensor", 0)
    new_keys = jnp.where(parity == 0, own_half, other_half)[:, None, :]
    new_values = jnp.where(parity == 0, other_half, own_half)[:, None, :]
    local_pool = page_pool[None]
    own_grouped = own_q.reshape(row_count, kv_local, local_q // kv_local, HD)
    other_q = partner(own_q, "tensor", 0)
    lower_first = jnp.concatenate([own_q, other_q], axis=1)
    upper_first = jnp.concatenate([other_q, own_q], axis=1)
    group_q = jnp.where(parity == 0, lower_first, upper_first).reshape(row_count, 1, group, HD)
    found = cached_all(
        group_q,
        local_pool,
        parity * page_pool.shape[0],
        page_table,
        prefill_offsets,
        decode_lengths,
        C,
    )
    low_part = tuple((piece[:, :, :local_q] for piece in found))
    high_part = tuple((piece[:, :, local_q:] for piece in found))
    mine = tuple(
        (
            jnp.where(parity == 0, low_piece, high_piece)
            for low_piece, high_piece in zip(low_part, high_part)
        )
    )
    theirs = tuple(
        (
            jnp.where(parity == 0, high_piece, low_piece)
            for low_piece, high_piece in zip(low_part, high_part)
        )
    )
    received = partner((theirs[0], theirs[1], theirs[2]), "tensor", 0)
    cached = combine_parts(mine, received)
    fresh = fresh_all(own_grouped, new_keys, new_values, C)
    highest, totals, blended = combine_parts(cached, fresh)
    attended = (blended / totals[..., None]).astype(jnp.bfloat16).reshape(row_count, local_q * HD)
    piece = attended
    summed = lax.psum_scatter(
        jnp.dot(piece, output_weight, preferred_element_type=jnp.float32),
        "tensor",
        scatter_dimension=0,
        tiled=True,
    )
    return summed.astype(jnp.bfloat16)


def solution(mesh):
    placed = (
        P(("req", "tensor"), None),
        P(),
        P(None, "tensor"),
        P(None, "tensor"),
        P("tensor", None),
        P(("req", "tensor"), None, None),
        P("req", None),
        P("req"),
        P("req"),
    )
    return jax.shard_map(
        shards, mesh=mesh, in_specs=placed, out_specs=P(("req", "tensor"), None), check_vma=False
    )
```

profile of v0, /device:TPU:160, one launch (start us, length us, event | category | flops | bytes accessed | tf_op | source)
XLA Modules:
  0.0 436.9 jit_solution(1664595664184705682)
XLA Ops:
  17.4 5.5 %fusion.116 = pred[1024]{0:T(1024)(128)(4,1)S(1)} fusion(s32[]{:T(128)} %bitcast.35, pred[]{:T(512)} %bitcast.34, pred[]{:T(512)} %bitcast.33, pred[]{:T(512)} %bitcast.32, pred[]{:T(512)} %bitcast.31, pred[]{:T(512)} %bitcast.30, pred[]{:T(512)} %bitcast.29, pred[]{:T(512)} %bitcast.28, pred[]{:T(512)} %bitcast.27), kind=kLoop, calls=%fused_computation.187 | loop fusion | flops 25600 | bytes 1036 | tf_op jit(solution)/shard_map/and | solution.py:49
  23.0 5.6 %fusion.117 = pred[1024]{0:T(1024)(128)(4,1)S(1)} fusion(s32[]{:T(128)} %bitcast.42, pred[]{:T(512)} %bitcast.54, pred[]{:T(512)} %bitcast.53, pred[]{:T(512)} %bitcast.52, pred[]{:T(512)} %bitcast.51, pred[]{:T(512)} %bitcast.50, pred[]{:T(512)} %bitcast.49, pred[]{:T(512)} %bitcast.48, pred[]{:T(512)} %bitcast.47), kind=kLoop, calls=%fused_computation.188 | loop fusion | flops 25600 | bytes 1036 | tf_op jit(solution)/shard_map/and | solution.py:49
  33.6 55.6 %all-gather.2.cloned.1.call-done = bf16[512,8192]{1,0:T(8,128)(2,1)} async-done(((bf16[32,8192]{1,0:T(8,128)(2,1)}), bf16[512,8192]{1,0:T(8,128)(2,1)}) %all-gather.2.cloned.1.call-update) | async-done | bytes 8388624 | tf_op jit(solution)/shard_map/all_gather | solution.py:172
  89.2 6.9 %fusion.141 = f32[512,256]{0,1:T(8,128)S(1)} fusion(bf16[512,8192]{1,0:T(8,128)(2,1)} %all-gather.2.cloned.1.call-done, bf16[8192,256]{1,0:T(8,128)(2,1)} %param.23), kind=kOutput, calls=%fused_computation.227 | convolution fusion | flops 2147483648 | bytes 13107200 | tf_op jit(solution)/shard_map/dot_general | solution.py:175
  96.4 5.7 %fusion.142 = f32[512,128]{1,0:T(8,128)S(1)} fusion(bf16[512,8192]{1,0:T(8,128)(2,1)} %all-gather.2.cloned.1.call-done, bf16[8192,128]{1,0:T(8,128)(2,1)S(1)} %copy-done), kind=kOutput, calls=%fused_computation.228 | convolution fusion | flops 1073741824 | bytes 10747904 | tf_op jit(solution)/shard_map/dot_general | solution.py:176
  125.4 134.0 %while.21 = (s32[]{:T(128)}, f32[16,1,1,4]{3,2,1,0:T(1,128)S(1)}, f32[16,1,1,4]{3,2,1,0:T(1,128)S(1)}, f32[16,1,1,4,128]{4,0,3,2,1:T(8,128)S(1)}, s32[16,8]{1,0:...) while((s32[]{:T(128)}, f32[16,1,1,4]{3,2,1,0:T(1,128)S(1)}, ...), condition=%wide.region_6.9_spmd, body=%wide.region_3.8_spmd.sunk | while | flops 2422874 | bytes 2688929 | solution.py:88
  126.8 5.5 %fusion.158 = pred[1024]{0:T(1024)(128)(4,1)S(1)} fusion(s32[]{:T(128)} %bitcast.422, pred[]{:T(512)} %bitcast.423, pred[]{:T(512)} %bitcast.424, pred[]{:T(512)} %bitcast.425, pred[]{:T(512)} %bitcast.426, pred[]{:T(512)} %bitcast.427, pred[]{:T(512)} %bitcast.428, pred[]{:T(512)} %bitcast.429, pred[]{:T(512)} %bitcast.430), kind=kLoop, calls=%fused_computation.37.clone.1 | loop fusion | flops 25600 | bytes 1036 | tf_op jit(solution)/shard_map/while/body/eval_jaxpr/and | solution.py:49
  135.1 5.5 %fusion.158 = pred[1024]{0:T(1024)(128)(4,1)S(1)} fusion(s32[]{:T(128)} %bitcast.422, pred[]{:T(512)} %bitcast.423, pred[]{:T(512)} %bitcast.424, pred[]{:T(512)} %bitcast.425, pred[]{:T(512)} %bitcast.426, pred[]{:T(512)} %bitcast.427, pred[]{:T(512)} %bitcast.428, pred[]{:T(512)} %bitcast.429, pred[]{:T(512)} %bitcast.430), kind=kLoop, calls=%fused_computation.37.clone.1 | loop fusion | flops 25600 | bytes 1036 | tf_op jit(solution)/shard_map/while/body/eval_jaxpr/and | solution.py:49
  143.5 5.5 %fusion.158 = pred[1024]{0:T(1024)(128)(4,1)S(1)} fusion(s32[]{:T(128)} %bitcast.422, pred[]{:T(512)} %bitcast.423, pred[]{:T(512)} %bitcast.424, pred[]{:T(512)} %bitcast.425, pred[]{:T(512)} %bitcast.426, pred[]{:T(512)} %bitcast.427, pred[]{:T(512)} %bitcast.428, pred[]{:T(512)} %bitcast.429, pred[]{:T(512)} %bitcast.430), kind=kLoop, calls=%fused_computation.37.clone.1 | loop fusion | flops 25600 | bytes 1036 | tf_op jit(solution)/shard_map/while/body/eval_jaxpr/and | solution.py:49
  151.9 5.5 %fusion.158 = pred[1024]{0:T(1024)(128)(4,1)S(1)} fusion(s32[]{:T(128)} %bitcast.422, pred[]{:T(512)} %bitcast.423, pred[]{:T(512)} %bitcast.424, pred[]{:T(512)} %bitcast.425, pred[]{:T(512)} %bitcast.426, pred[]{:T(512)} %bitcast.427, pred[]{:T(512)} %bitcast.428, pred[]{:T(512)} %bitcast.429, pred[]{:T(512)} %bitcast.430), kind=kLoop, calls=%fused_computation.37.clone.1 | loop fusion | flops 25600 | bytes 1036 | tf_op jit(solution)/shard_map/while/body/eval_jaxpr/and | solution.py:49
  160.2 5.5 %fusion.158 = pred[1024]{0:T(1024)(128)(4,1)S(1)} fusion(s32[]{:T(128)} %bitcast.422, pred[]{:T(512)} %bitcast.423, pred[]{:T(512)} %bitcast.424, pred[]{:T(512)} %bitcast.425, pred[]{:T(512)} %bitcast.426, pred[]{:T(512)} %bitcast.427, pred[]{:T(512)} %bitcast.428, pred[]{:T(512)} %bitcast.429, pred[]{:T(512)} %bitcast.430), kind=kLoop, calls=%fused_computation.37.clone.1 | loop fusion | flops 25600 | bytes 1036 | tf_op jit(solution)/shard_map/while/body/eval_jaxpr/and | solution.py:49
  168.6 5.5 %fusion.158 = pred[1024]{0:T(1024)(128)(4,1)S(1)} fusion(s32[]{:T(128)} %bitcast.422, pred[]{:T(512)} %bitcast.423, pred[]{:T(512)} %bitcast.424, pred[]{:T(512)} %bitcast.425, pred[]{:T(512)} %bitcast.426, pred[]{:T(512)} %bitcast.427, pred[]{:T(512)} %bitcast.428, pred[]{:T(512)} %bitcast.429, pred[]{:T(512)} %bitcast.430), kind=kLoop, calls=%fused_computation.37.clone.1 | loop fusion | flops 25600 | bytes 1036 | tf_op jit(solution)/shard_map/while/body/eval_jaxpr/and | solution.py:49
  177.0 5.5 %fusion.158 = pred[1024]{0:T(1024)(128)(4,1)S(1)} fusion(s32[]{:T(128)} %bitcast.422, pred[]{:T(512)} %bitcast.423, pred[]{:T(512)} %bitcast.424, pred[]{:T(512)} %bitcast.425, pred[]{:T(512)} %bitcast.426, pred[]{:T(512)} %bitcast.427, pred[]{:T(512)} %bitcast.428, pred[]{:T(512)} %bitcast.429, pred[]{:T(512)} %bitcast.430), kind=kLoop, calls=%fused_computation.37.clone.1 | loop fusion | flops 25600 | bytes 1036 | tf_op jit(solution)/shard_map/while/body/eval_jaxpr/and | solution.py:49
  185.4 5.5 %fusion.158 = pred[1024]{0:T(1024)(128)(4,1)S(1)} fusion(s32[]{:T(128)} %bitcast.422, pred[]{:T(512)} %bitcast.423, pred[]{:T(512)} %bitcast.424, pred[]{:T(512)} %bitcast.425, pred[]{:T(512)} %bitcast.426, pred[]{:T(512)} %bitcast.427, pred[]{:T(512)} %bitcast.428, pred[]{:T(512)} %bitcast.429, pred[]{:T(512)} %bitcast.430), kind=kLoop, calls=%fused_computation.37.clone.1 | loop fusion | flops 25600 | bytes 1036 | tf_op jit(solution)/shard_map/while/body/eval_jaxpr/and | solution.py:49
  193.7 5.5 %fusion.158 = pred[1024]{0:T(1024)(128)(4,1)S(1)} fusion(s32[]{:T(128)} %bitcast.422, pred[]{:T(512)} %bitcast.423, pred[]{:T(512)} %bitcast.424, pred[]{:T(512)} %bitcast.425, pred[]{:T(512)} %bitcast.426, pred[]{:T(512)} %bitcast.427, pred[]{:T(512)} %bitcast.428, pred[]{:T(512)} %bitcast.429, pred[]{:T(512)} %bitcast.430), kind=kLoop, calls=%fused_computation.37.clone.1 | loop fusion | flops 25600 | bytes 1036 | tf_op jit(solution)/shard_map/while/body/eval_jaxpr/and | solution.py:49
  202.1 5.5 %fusion.158 = pred[1024]{0:T(1024)(128)(4,1)S(1)} fusion(s32[]{:T(128)} %bitcast.422, pred[]{:T(512)} %bitcast.423, pred[]{:T(512)} %bitcast.424, pred[]{:T(512)} %bitcast.425, pred[]{:T(512)} %bitcast.426, pred[]{:T(512)} %bitcast.427, pred[]{:T(512)} %bitcast.428, pred[]{:T(512)} %bitcast.429, pred[]{:T(512)} %bitcast.430), kind=kLoop, calls=%fused_computation.37.clone.1 | loop fusion | flops 25600 | bytes 1036 | tf_op jit(solution)/shard_map/while/body/eval_jaxpr/and | solution.py:49
  210.5 5.5 %fusion.158 = pred[1024]{0:T(1024)(128)(4,1)S(1)} fusion(s32[]{:T(128)} %bitcast.422, pred[]{:T(512)} %bitcast.423, pred[]{:T(512)} %bitcast.424, pred[]{:T(512)} %bitcast.425, pred[]{:T(512)} %bitcast.426, pred[]{:T(512)} %bitcast.427, pred[]{:T(512)} %bitcast.428, pred[]{:T(512)} %bitcast.429, pred[]{:T(512)} %bitcast.430), kind=kLoop, calls=%fused_computation.37.clone.1 | loop fusion | flops 25600 | bytes 1036 | tf_op jit(solution)/shard_map/while/body/eval_jaxpr/and | solution.py:49
  218.9 5.5 %fusion.158 = pred[1024]{0:T(1024)(128)(4,1)S(1)} fusion(s32[]{:T(128)} %bitcast.422, pred[]{:T(512)} %bitcast.423, pred[]{:T(512)} %bitcast.424, pred[]{:T(512)} %bitcast.425, pred[]{:T(512)} %bitcast.426, pred[]{:T(512)} %bitcast.427, pred[]{:T(512)} %bitcast.428, pred[]{:T(512)} %bitcast.429, pred[]{:T(512)} %bitcast.430), kind=kLoop, calls=%fused_computation.37.clone.1 | loop fusion | flops 25600 | bytes 1036 | tf_op jit(solution)/shard_map/while/body/eval_jaxpr/and | solution.py:49
  227.2 5.5 %fusion.158 = pred[1024]{0:T(1024)(128)(4,1)S(1)} fusion(s32[]{:T(128)} %bitcast.422, pred[]{:T(512)} %bitcast.423, pred[]{:T(512)} %bitcast.424, pred[]{:T(512)} %bitcast.425, pred[]{:T(512)} %bitcast.426, pred[]{:T(512)} %bitcast.427, pred[]{:T(512)} %bitcast.428, pred[]{:T(512)} %bitcast.429, pred[]{:T(512)} %bitcast.430), kind=kLoop, calls=%fused_computation.37.clone.1 | loop fusion | flops 25600 | bytes 1036 | tf_op jit(solution)/shard_map/while/body/eval_jaxpr/and | solution.py:49
  235.6 5.5 %fusion.158 = pred[1024]{0:T(1024)(128)(4,1)S(1)} fusion(s32[]{:T(128)} %bitcast.422, pred[]{:T(512)} %bitcast.423, pred[]{:T(512)} %bitcast.424, pred[]{:T(512)} %bitcast.425, pred[]{:T(512)} %bitcast.426, pred[]{:T(512)} %bitcast.427, pred[]{:T(512)} %bitcast.428, pred[]{:T(512)} %bitcast.429, pred[]{:T(512)} %bitcast.430), kind=kLoop, calls=%fused_computation.37.clone.1 | loop fusion | flops 25600 | bytes 1036 | tf_op jit(solution)/shard_map/while/body/eval_jaxpr/and | solution.py:49
  244.0 5.5 %fusion.158 = pred[1024]{0:T(1024)(128)(4,1)S(1)} fusion(s32[]{:T(128)} %bitcast.422, pred[]{:T(512)} %bitcast.423, pred[]{:T(512)} %bitcast.424, pred[]{:T(512)} %bitcast.425, pred[]{:T(512)} %bitcast.426, pred[]{:T(512)} %bitcast.427, pred[]{:T(512)} %bitcast.428, pred[]{:T(512)} %bitcast.429, pred[]{:T(512)} %bitcast.430), kind=kLoop, calls=%fused_computation.37.clone.1 | loop fusion | flops 25600 | bytes 1036 | tf_op jit(solution)/shard_map/while/body/eval_jaxpr/and | solution.py:49
  252.4 5.5 %fusion.158 = pred[1024]{0:T(1024)(128)(4,1)S(1)} fusion(s32[]{:T(128)} %bitcast.422, pred[]{:T(512)} %bitcast.423, pred[]{:T(512)} %bitcast.424, pred[]{:T(512)} %bitcast.425, pred[]{:T(512)} %bitcast.426, pred[]{:T(512)} %bitcast.427, pred[]{:T(512)} %bitcast.428, pred[]{:T(512)} %bitcast.429, pred[]{:T(512)} %bitcast.430), kind=kLoop, calls=%fused_computation.37.clone.1 | loop fusion | flops 25600 | bytes 1036 | tf_op jit(solution)/shard_map/while/body/eval_jaxpr/and | solution.py:49
  264.5 10.3 %fusion.143 = f32[512,8192]{1,0:T(8,128)} fusion(bf16[512,256]{0,1:T(8,128)(2,1)S(1)} %bitcast.441, bf16[256,8192]{1,0:T(8,128)(2,1)} %param.25), kind=kOutput, calls=%fused_computation.229 | convolution fusion | flops 2147483648 | bytes 21233664 | tf_op jit(solution)/shard_map/dot_general | solution.py:231
  274.8 153.3 %reduce-scatter.2.cloned.1.call-done = f32[32,8192]{1,0:T(8,128)} async-done(((f32[512,8192]{1,0:T(8,128)}), f32[32,8192]{1,0:T(8,128)}) %reduce-scatter.2.cloned.1.call-update) | async-done | bytes 1048592 | tf_op jit(solution)/shard_map/reduce_scatter | solution.py:230
  (299 shorter events, 90.7 us)
Async XLA Ops:
  6.5 89.9 %copy-start = (bf16[8192,128]{1,0:T(8,128)(2,1)S(1)}, bf16[8192,128]{1,0:T(8,128)(2,1)}, u32[]{:S(2)}) copy-start(bf16[8192,128]{1,0:T(8,128)(2,1)} %param.24) | copy-start | bytes 6291460
  6.5 10.0 %copy-start.5 = (s32[18,8]{0,1:T(8,128)S(1)}, s32[18,8]{0,1:T(8,128)}, u32[]{:S(2)}) copy-start(s32[18,8]{0,1:T(8,128)} %param.27) | copy-start | bytes 1732
  6.5 9.4 %copy-start.7 = (s32[2]{0:T(128)S(1)}, s32[2]{0:T(128)}, u32[]{:S(2)}) copy-start(s32[2]{0:T(128)} %param.28) | copy-start | bytes 28
  6.5 23.2 %copy-start.10 = (s32[16]{0:T(128)S(1)}, s32[16]{0:T(128)}, u32[]{:S(2)}) copy-start(s32[16]{0:T(128)} %param.29) | copy-start | bytes 196
  6.5 82.6 %all-gather.2.cloned.1.call-start = ((), (), s32[]{:S(2)}) async-start(), calls=%async_computation.1 | async-start | bytes 8912896 | tf_op jit(solution)/shard_map/all_gather | solution.py:172
  10.0 418.0 %reduce-scatter.2.cloned.1.call-start = ((), (), s32[]{:S(2)}) async-start(), calls=%async_computation.2 | async-start | bytes 17825792 | tf_op jit(solution)/shard_map/reduce_scatter | solution.py:230
  15.9 13.9 %copy-start.8 = (f32[64]{0:T(128)}, f32[64]{0:T(128)S(1)}, u32[]{:S(2)}) copy-start(f32[64]{0:T(128)S(1)} %multiply_power_fusion) | copy-start | bytes 772
  96.4 5.7 %copy-start.9 = (f32[64]{0:T(128)S(1)}, f32[64]{0:T(128)}, u32[]{:S(2)}) copy-start(f32[64]{0:T(128)} %copy-done.8) | copy-start | bytes 772
  104.1 3.7 collective-permute-start.2
  107.5 8.9 %collective-permute-start = (bf16[512,2,128]{2,0,1:T(8,128)(2,1)}, bf16[512,2,128]{2,0,1:T(8,128)(2,1)}, u32[]{:S(2)}, u32[]{:S(2)}) collective-permute-start(bf16[512,2,128]{2,0,1:T(8,128)(2,1)} %pad_maximum_fusion.1), channel_id=1, source_target_pairs={{0,1},{1,0},{2,3},{3,2},{4,5},{5,4},{6,7},{7,6},{8,9},{9,8},{10,11... | collective-permute-start | bytes 786440 | tf_op jit(solution)/shard_map/ppermute | solution.py:18
  111.1 6.6 %copy-start.3 = (bf16[1,8,128,256]{3,2,1,0:T(8,128)(2,1)S(1)}, bf16[1,8,128,256]{3,2,1,0:T(8,128)(2,1)}, u32[]{:S(2)}) copy-start(bf16[1,8,128,256]{3,2,1,0:T(8,128)(2,1)} %bitcast_select_fusion.3) | copy-start | bytes 1572868
  118.5 3.0 copy-start.2
  122.4 3.0 copy-start.1
  122.4 3.0 copy-start.11
  125.4 137.9 %copy-start.6 = (f32[512]{0:T(512)S(1)}, f32[512]{0:T(512)}, u32[]{:S(2)}) copy-start(f32[512]{0:T(512)} %pad.16.clone) | copy-start | bytes 6148
  259.4 4.0 copy-start.4
  259.6 2.7 collective-permute-start.1
  261.3 2.1 collective-permute-start.3
  261.7 1.6 collective-permute-start.4
Sparse Core Ops, SparseCore 0:
  10.2 78.9 all-gather.1
  274.9 153.0 reduce-scatter.1
where the time goes:
time: 441 us; the launch traced here: 437 us
  waiting for transfers between devices  210 us (48%)
  other arithmetic  131 us (30%)
  matrix products  41.2 us (9%)
  local copies, waits for them, and re-layouts  38.4 us (9%)
  between operations  13.8 us (3%)
    reduce_scatter x1, waiting for transfers between devices, shards(): lax.psum_scatter(jnp.dot(piece, output_weight, preferred_element_type=jnp...  153 us
    and x18, other arithmetic, cached_block(): jnp.repeat(owned_page, page_len, total_repeat_length=key_span)  99.7 us
    all_gather x1, waiting for transfers between devices, shards(): project_piece = lax.all_gather(normed, 'tensor', axis=0, tiled=True)  55.6 us
    gather x18, local copies, waits for them, and re-layouts, cached_block(): fetched = jnp.take(pool_rows, local_page, axis=1)  12.5 us
    gather x17, local copies, waits for them, and re-layouts, cached_block(): jnp.repeat(owned_page, page_len, total_repeat_length=key_span)  11.4 us
    dot_general x1, matrix products, shards(): jnp.dot(piece, output_weight, preferred_element_type=jnp.float32)  10.3 us
    dynamic_slice x16, local copies, waits for them, and re-layouts, cached_all(): lax.map(decode_one, (queries[2 * stretch_len:], page_table[2:], decode_le...  9.91 us
  transfers between devices with their start and end apart: 7, of which 3 were waited for; matrix products, arithmetic and copies ran while one was open for 8% of the time, Pallas kernels for 0%

commit v1 on v0

v1 whole, which is shorter than its diff:
```python
import functools

import jax
import jax.numpy as jnp
import numpy as np
from jax import lax
from jax.experimental import pallas as pl
from jax.experimental.pallas import tpu as pltpu
from jax.sharding import PartitionSpec as P

HD = 128
C = 248
PAGE = 128
MAXP = 8
ROWS = 512
D = 8192
CW = 1024
NC = D // CW
CA = 640
eps_norm = 1e-06
rope_base = 1000000.0
neg_big = -1e30
MESH = pl.DeviceIdType.MESH
F32 = jnp.float32
BF16 = jnp.bfloat16
B_LO = 112
B_ROWS = 256 - B_LO
SPAN = MAXP * PAGE


def kernel(
    x_ref, gain_ref, freq_ref, wq_hbm, wkv_hbm, wo_hbm, pool_hbm, table_ref, off_ref, len_ref,
    out_ref,
    xg, w, wo, pool, kvc, acc, newkv, qa, qb, qd, trig, sa, sb, sd, pa, pb, pd, la, lb, cnt, att,
    pbuf, r_al, r_ar, r_l, r_r, r_y, s_y, s_al, s_ar, s_l, s_r,
    own_sem, ws_sem, wr_sem, ag_s, ag_r, kv_s, kv_r, rs_s, rs_r,
):
    req = lax.axis_index("req")
    me = lax.axis_index("tensor")
    h, x, c = me // 8, (me // 2) % 4, me % 2

    def dev(hh, xx, cc):
        return (req, hh * 8 + xx * 2 + cc)

    xr, xl, xo = lax.rem(x + 1, 4), lax.rem(x + 3, 4), lax.rem(x + 2, 4)
    core_dev, right, left, across = dev(h, x, 1 - c), dev(h, xr, c), dev(h, xl, c), dev(1 - h, x, c)

    def send(src, dst, ssem, rsem, to):
        return pltpu.make_async_remote_copy(
            src_ref=src, dst_ref=dst, send_sem=ssem, recv_sem=rsem, device_id=to, device_id_type=MESH
        )

    qcol = pl.multiple_of(c * 256, 256)
    kcol = pl.multiple_of(512 + c * 128, 128)
    orow = pl.multiple_of(c * 256, 256)
    prow = c * 8
    own = [
        pltpu.make_async_copy(pool_hbm, pool.at[pl.ds(prow, 8)], own_sem.at[0]),
        pltpu.make_async_copy(wq_hbm, w.at[:, pl.ds(qcol, 256)], own_sem.at[1]),
        pltpu.make_async_copy(wkv_hbm, w.at[:, pl.ds(kcol, 128)], own_sem.at[2]),
        pltpu.make_async_copy(wo_hbm, wo.at[pl.ds(orow, 256)], own_sem.at[3]),
    ]
    for copy in own:
        copy.start()

    barrier = pltpu.get_barrier_semaphore()
    for to in (core_dev, right, left, across):
        pl.semaphore_signal(barrier, inc=1, device_id=to, device_id_type=MESH)

    mine = pl.multiple_of((h * 4 + x) * 32, 32)
    total = jnp.zeros((32, 1), F32)
    for i in range(NC):
        v = x_ref[:, i * CW : (i + 1) * CW].astype(F32)
        total = total + jnp.sum(v * v, axis=1, keepdims=True)
    inv = lax.rsqrt(total * (1.0 / D) + eps_norm)
    for i in range(NC):
        v = x_ref[:, i * CW : (i + 1) * CW].astype(F32)
        xg[i, pl.ds(mine, 32), :] = (v * inv * gain_ref[:, i * CW : (i + 1) * CW]).astype(BF16)

    pl.semaphore_wait(barrier, 4)

    swap_pool = send(pool_hbm, pool.at[pl.ds(prow, 8)], ws_sem.at[0], wr_sem.at[0], core_dev)
    swap_wo = send(wo_hbm, wo.at[pl.ds(orow, 256)], ws_sem.at[1], wr_sem.at[1], core_dev)

    def swap_q(i):
        r = pl.ds(pl.multiple_of(i * CW, CW), CW)
        return send(wq_hbm.at[r], w.at[r, pl.ds(qcol, 256)], ws_sem.at[2 + i], wr_sem.at[2 + i], core_dev)

    def swap_kv(i):
        r = pl.ds(pl.multiple_of(i * CW, CW), CW)
        return send(
            wkv_hbm.at[r], w.at[r, pl.ds(kcol, 128)], ws_sem.at[2 + NC + i], wr_sem.at[2 + NC + i], core_dev
        )

    def block(hh, xx):
        return pl.multiple_of((hh * 4 + xx) * 32, 32)

    b_own, b_par = block(h, x), block(1 - h, x)
    b_l, b_r, b_o = block(h, xl), block(h, xr), block(h, xo)
    p_l, p_r = block(1 - h, xl), block(1 - h, xr)

    def part(k, i, row, n, lo, hi, to):
        ref = xg.at[i, pl.ds(pl.multiple_of(row, 16), n), lo:hi]
        return send(ref, ref, ag_s.at[i, k], ag_r.at[i, k], to)

    def gather(k, i):
        if k == 0:
            return part(k, i, b_own, 32, 0, CA, across)
        if k == 1:
            return part(k, i, b_own, 32, 0, CA, right)
        if k == 2:
            return part(k, i, b_own, 32, 0, CA, left)
        if k == 3:
            return part(k, i, b_par, 32, 0, CA, right)
        if k == 4:
            return part(k, i, b_par, 32, 0, CA, left)
        if k == 5:
            return part(k, i, b_l, 16, 0, CA, right)
        if k == 6:
            return part(k, i, b_r + 16, 16, 0, CA, left)
        if k == 7:
            return part(k, i, p_l, 16, 0, CA, right)
        if k == 8:
            return part(k, i, p_r + 16, 16, 0, CA, left)
        if k == 9:
            return part(k, i, b_own, 32, CA, CW, right)
        if k == 10:
            return part(k, i, b_own, 32, CA, CW, left)
        if k == 11:
            return part(k, i, b_own, 32, CA, CW, across)
        if k == 12:
            return part(k, i, b_l, 16, CA, CW, right)
        if k == 13:
            return part(k, i, b_r + 16, 16, CA, CW, left)
        if k == 14:
            return part(k, i, b_l, 32, CA, CW, across)
        if k == 15:
            return part(k, i, b_r, 32, CA, CW, across)
        return part(k, i, b_o, 32, CA, CW, across)

    swap_pool.start()
    acc[...] = jnp.zeros_like(acc)
    own[0].wait()
    own[1].wait()
    own[2].wait()

    def gather_step(s, carry):
        @pl.when(s < NC)
        def _():
            for k in (0, 1, 2, 9, 10, 11):
                gather(k, s).start()
            swap_q(s).start()
            swap_kv(s).start()

        @pl.when((s >= 1) & (s < NC + 1))
        def _():
            i = s - 1
            gather(0, i).wait_recv()
            gather(3, i).start()
            gather(4, i).start()
            gather(9, i).wait_recv()
            gather(12, i).start()
            gather(14, i).start()
            gather(10, i).wait_recv()
            gather(13, i).start()
            gather(15, i).start()
            gather(1, i).wait_recv()
            gather(5, i).start()
            gather(2, i).wait_recv()
            gather(6, i).start()

        @pl.when((s >= 2) & (s < NC + 2))
        def _():
            i = s - 2
            gather(12, i).wait_recv()
            gather(13, i).wait_recv()
            gather(16, i).start()
            gather(3, i).wait_recv()
            gather(7, i).start()
            gather(4, i).wait_recv()
            gather(8, i).start()

        @pl.when(s == 3)
        def _():
            prepare()

        @pl.when(s >= 3)
        def _():
            i = s - 3
            for k in (5, 6, 7, 8, 11, 14, 15, 16):
                gather(k, i).wait_recv()
            swap_q(i).wait_recv()
            swap_kv(i).wait_recv()
            r = pl.ds(pl.multiple_of(i * CW, CW), CW)
            acc[...] += jnp.dot(xg[i], w[r, :], preferred_element_type=F32)

        return carry

    def prepare():
        swap_pool.wait_recv()
        swap_wo.start()
        for st in range(2):
            for j in range(MAXP):
                kvc[st, j * PAGE : (j + 1) * PAGE, :] = pool[table_ref[st, j]]
        slot = lax.broadcasted_iota(jnp.int32, (16, 2048), 1)
        page, inside = slot // PAGE, slot % PAGE
        rid = lax.broadcasted_iota(jnp.int32, (16, 1), 0)
        length = jnp.zeros((16, 1), jnp.int32)
        for b in range(16):
            length = jnp.where(rid == b, len_ref[b], length)
        count = jnp.zeros((16, 2048), F32)
        for j in range(MAXP):
            named = jnp.zeros((16, 1), jnp.int32)
            for b in range(16):
                named = jnp.where(rid == b, table_ref[2 + b, j], named)
            seen = (page == named) & (inside + j * PAGE < length)
            count = count + jnp.where(seen, 1.0, 0.0)
        cnt[...] = count
        lr = lax.broadcasted_iota(jnp.int32, (256, 1), 0)
        g = ((lr // 32) * 2 + c) * 32 + lr % 32
        position = jnp.where(g < C, off_ref[0] + g, off_ref[1] + g - C)
        for b in range(16):
            position = jnp.where(g == 2 * C + b, len_ref[b], position)
        angle = position.astype(F32) * freq_ref[...]
        lane = lax.broadcasted_iota(jnp.int32, (256, HD), 1)
        trig[0] = jnp.cos(angle)
        trig[1] = jnp.where(lane < HD // 2, -jnp.sin(angle), jnp.sin(angle))

    lax.fori_loop(0, NC + 3, gather_step, 0)

    def rotated(col):
        v = acc[:, col : col + HD]
        return (v * trig[0] + pltpu.roll(v, HD // 2, 1) * trig[1]).astype(BF16)

    base = pl.multiple_of(c * 256, 256)
    newkv[pl.ds(base, 256), 0:HD] = rotated(512)
    newkv[pl.ds(base, 256), HD : 2 * HD] = acc[:, 640:768].astype(BF16)
    for n in range(4):
        q = rotated(n * HD)
        qa[n * 128 : (n + 1) * 128, :] = q[0:128]
        qb[n * B_ROWS : (n + 1) * B_ROWS, :] = q[B_LO:256]
        qd[n * 16 : (n + 1) * 16, :] = q[240:256]
        if n == 0:
            kv_part = newkv.at[pl.ds(base, 256)]
            swap_new = send(kv_part, kv_part, kv_s, kv_r, core_dev)
            swap_new.start()

    def nt(a, b):
        return lax.dot_general(a, b, (((1,), (1,)), ((), ())), preferred_element_type=F32)

    sa[:, 0:SPAN] = nt(qa[...], kvc[0, :, 0:HD])
    sb[:, 0:SPAN] = nt(qb[...], kvc[1, :, 0:HD])
    swap_new.wait_recv()
    sa[:, SPAN : SPAN + 128] = nt(qa[...], newkv[0:128, 0:HD])
    sa[:, SPAN + 128 : SPAN + 256] = nt(qa[...], newkv[256:384, 0:HD])
    sb[:, SPAN : SPAN + 384] = nt(qb[...], newkv[128:512, 0:HD])
    scale = HD ** (-0.5)

    def globals_of(lr):
        return ((lr // 32) * 2 + c) * 32 + lr % 32

    def key_globals(row):
        lr = row % 256
        return ((lr // 32) * 2 + row // 256) * 32 + lr % 32

    def softmax(s_ref, p_ref, l_ref, r0, n, q_glob, key_glob, floor, width, limit):
        rows = pl.ds(pl.multiple_of(r0, 16), n)
        slots = lax.broadcasted_iota(jnp.int32, (1, SPAN), 1)
        sc = jnp.where(slots < limit, s_ref[rows, 0:SPAN], neg_big)
        sn = jnp.where(
            (key_glob <= q_glob) & (key_glob >= floor), s_ref[rows, SPAN : SPAN + width], neg_big
        )
        m = jnp.maximum(jnp.max(sc, axis=1, keepdims=True), jnp.max(sn, axis=1, keepdims=True))
        ec = jnp.exp((sc - m) * scale)
        en = jnp.exp((sn - m) * scale)
        l_ref[rows, :] = jnp.broadcast_to(
            jnp.sum(ec, axis=1, keepdims=True) + jnp.sum(en, axis=1, keepdims=True), (n, HD)
        )
        p_ref[rows, 0:SPAN] = ec.astype(BF16)
        p_ref[rows, SPAN : SPAN + width] = en.astype(BF16)

    def soft_a(b, carry):
        r0 = b * 32
        lr = lax.rem(r0, 128) + lax.broadcasted_iota(jnp.int32, (32, 1), 0)
        k = lax.broadcasted_iota(jnp.int32, (1, 256), 1)
        kg = key_globals(jnp.where(k < 128, k, k + 128))
        kg = jnp.where(kg < C, kg, 2 * ROWS)
        softmax(sa, pa, la, r0, 32, globals_of(lr), kg, 0, 256, off_ref[0])
        return carry

    def soft_b(b, carry):
        r0 = b * 48
        lr = B_LO + lax.rem(r0, B_ROWS) + lax.broadcasted_iota(jnp.int32, (48, 1), 0)
        k = lax.broadcasted_iota(jnp.int32, (1, 384), 1)
        softmax(sb, pb, lb, r0, 48, globals_of(lr), key_globals(k + 128), C, 384, off_ref[1])
        return carry

    lax.fori_loop(0, 16, soft_a, 0)
    oa = jnp.dot(pa[:, 0:SPAN], kvc[0, :, HD : 2 * HD], preferred_element_type=F32)
    oa = oa + jnp.dot(pa[:, SPAN : SPAN + 128], newkv[0:128, HD : 2 * HD], preferred_element_type=F32)
    oa = oa + jnp.dot(pa[:, SPAN + 128 : SPAN + 256], newkv[256:384, HD : 2 * HD], preferred_element_type=F32)
    oa = (oa / la[...]).astype(BF16)
    for n in range(4):
        att[0:128, n * HD : (n + 1) * HD] = oa[n * 128 : (n + 1) * 128]
    lax.fori_loop(0, 12, soft_b, 0)
    ob = jnp.dot(pb[:, 0:SPAN], kvc[1, :, HD : 2 * HD], preferred_element_type=F32)
    ob = ob + jnp.dot(pb[:, SPAN : SPAN + 384], newkv[128:512, HD : 2 * HD], preferred_element_type=F32)
    ob = (ob / lb[...]).astype(BF16)
    near = lax.broadcasted_iota(jnp.int32, (16, 1), 0) >= 8 + 8 * (1 - c)
    for n in range(4):
        cols = slice(n * HD, (n + 1) * HD)
        att[128:256, cols] = ob[n * B_ROWS + 16 : (n + 1) * B_ROWS]
        att[B_LO:128, cols] = jnp.where(
            near, ob[n * B_ROWS : n * B_ROWS + 16].astype(F32), att[B_LO:128, cols].astype(F32)
        ).astype(BF16)

    @pl.when(c == 1)
    def _():
        for b in range(16):
            sd[:, b * 128 : (b + 1) * 128] = nt(qd[...], pool[b, :, 0:HD])
        self_s = nt(qd[...], newkv[496:512, 0:HD])
        kid = lax.broadcasted_iota(jnp.int32, (64, 16), 1)
        qid = lax.broadcasted_iota(jnp.int32, (64, 16), 0) % 16
        self_s = jnp.where(kid == qid, self_s, neg_big)
        for n in range(4):
            rows = slice(n * 16, (n + 1) * 16)
            own_s = self_s[n * 16 : (n + 1) * 16]
            count = cnt[...]
            s = jnp.where(count > 0.0, sd[rows, :], neg_big)
            m = jnp.maximum(jnp.max(s, axis=1, keepdims=True), jnp.max(own_s, axis=1, keepdims=True))
            e = count * jnp.exp((s - m) * scale)
            e_own = jnp.exp((own_s - m) * scale)
            tot = jnp.sum(e, axis=1, keepdims=True) + jnp.sum(e_own, axis=1, keepdims=True)
            pd[rows, :] = e.astype(BF16)
            o = jnp.dot(e_own.astype(BF16), newkv[496:512, HD : 2 * HD], preferred_element_type=F32)
            for b in range(16):
                o = o + jnp.dot(
                    pd[rows, b * 128 : (b + 1) * 128], pool[b, :, HD : 2 * HD], preferred_element_type=F32
                )
            att[240:256, n * HD : (n + 1) * HD] = (o / tot).astype(BF16)

    own[3].wait()
    swap_wo.wait_recv()

    def scatter(k, i):
        ss, rr = rs_s.at[i, k], rs_r.at[i, k]
        if k == 0:
            return send(pbuf.at[i, :, xo, 0:16, 0:CA], r_al.at[i], ss, rr, right)
        if k == 1:
            return send(pbuf.at[i, :, xo, 16:32, 0:CA], r_ar.at[i], ss, rr, left)
        if k == 2:
            return send(pbuf.at[i, :, xr, :, 0:CA], r_l.at[i], ss, rr, right)
        if k == 3:
            return send(pbuf.at[i, :, xl, :, 0:CA], r_r.at[i], ss, rr, left)
        if k == 4:
            return send(pbuf.at[i, 1 - h, x, :, 0:CA], r_y.at[i], ss, rr, across)
        if k == 5:
            return send(pbuf.at[i, 1 - h, :, :, CA:CW], s_y.at[i], ss, rr, across)
        if k == 6:
            return send(pbuf.at[i, h, xo, 0:16, CA:CW], s_al.at[i], ss, rr, right)
        if k == 7:
            return send(pbuf.at[i, h, xo, 16:32, CA:CW], s_ar.at[i], ss, rr, left)
        if k == 8:
            return send(pbuf.at[i, h, xr, :, CA:CW], s_l.at[i], ss, rr, right)
        return send(pbuf.at[i, h, xl, :, CA:CW], s_r.at[i], ss, rr, left)

    def f(v):
        return v.astype(F32)

    def scatter_step(s, carry):
        @pl.when(s < NC)
        def _():
            for b in range(CW // 256):
                col = pl.multiple_of(s * CW + b * 256, 256)
                prod = jnp.dot(att[...], wo[:, pl.ds(col, 256)], preferred_element_type=F32)
                pbuf[s, :, :, :, b * 256 : (b + 1) * 256] = prod.astype(BF16).reshape(2, 4, 32, 256)
            for k in (0, 1, 5):
                scatter(k, s).start()

        @pl.when((s >= 1) & (s < NC + 1))
        def _():
            i = s - 1
            scatter(0, i).wait_recv()
            pbuf[i, :, xr, 0:16, 0:CA] = (f(pbuf[i, :, xr, 0:16, 0:CA]) + f(r_al[i])).astype(BF16)
            scatter(1, i).wait_recv()
            pbuf[i, :, xl, 16:32, 0:CA] = (f(pbuf[i, :, xl, 16:32, 0:CA]) + f(r_ar[i])).astype(BF16)
            scatter(2, i).start()
            scatter(3, i).start()
            scatter(5, i).wait_recv()
            pbuf[i, h, :, :, CA:CW] = (f(pbuf[i, h, :, :, CA:CW]) + f(s_y[i])).astype(BF16)
            scatter(6, i).start()
            scatter(7, i).start()

        @pl.when((s >= 2) & (s < NC + 2))
        def _():
            i = s - 2
            scatter(2, i).wait_recv()
            scatter(3, i).wait_recv()
            pbuf[i, 1 - h, x, :, 0:CA] = (
                f(pbuf[i, 1 - h, x, :, 0:CA]) + f(r_l[i, 1 - h]) + f(r_r[i, 1 - h])
            ).astype(BF16)
            scatter(4, i).start()
            scatter(6, i).wait_recv()
            pbuf[i, h, xr, 0:16, CA:CW] = (f(pbuf[i, h, xr, 0:16, CA:CW]) + f(s_al[i])).astype(BF16)
            scatter(7, i).wait_recv()
            pbuf[i, h, xl, 16:32, CA:CW] = (f(pbuf[i, h, xl, 16:32, CA:CW]) + f(s_ar[i])).astype(BF16)
            scatter(8, i).start()
            scatter(9, i).start()

        @pl.when(s >= 3)
        def _():
            i = s - 3
            scatter(4, i).wait_recv()
            ca = pl.ds(pl.multiple_of(i * CW, 128), CA)
            cb = pl.ds(pl.multiple_of(i * CW + CA, 128), CW - CA)
            out_ref[:, ca] = (
                f(pbuf[i, h, x, :, 0:CA]) + f(r_l[i, h]) + f(r_r[i, h]) + f(r_y[i])
            ).astype(BF16)
            scatter(8, i).wait_recv()
            scatter(9, i).wait_recv()
            out_ref[:, cb] = (f(pbuf[i, h, x, :, CA:CW]) + f(s_l[i]) + f(s_r[i])).astype(BF16)

        return carry

    lax.fori_loop(0, NC + 3, scatter_step, 0)

    def drain(i, carry):
        for k in range(17):
            gather(k, i).wait_send()
        for k in range(10):
            scatter(k, i).wait_send()
        swap_q(i).wait_send()
        swap_kv(i).wait_send()
        return carry

    lax.fori_loop(0, NC, drain, 0)
    swap_pool.wait_send()
    swap_wo.wait_send()
    swap_new.wait_send()


def shards(x, gain, wq, wkv, wo, pool, table, offsets, lengths):
    half = np.arange(HD) % (HD // 2)
    freq = jnp.asarray((rope_base ** (-2.0 * half / HD)).astype(np.float32))[None]
    vmem = pl.BlockSpec(memory_space=pltpu.VMEM)
    smem = pl.BlockSpec(memory_space=pltpu.SMEM)
    anyw = pl.BlockSpec(memory_space=pl.ANY)
    cb = CW - CA
    dma = pltpu.SemaphoreType.DMA
    return pl.pallas_call(
        kernel,
        name="block",
        out_shape=jax.ShapeDtypeStruct((32, D), BF16),
        in_specs=[vmem, vmem, vmem, anyw, anyw, anyw, anyw, smem, smem, smem],
        out_specs=vmem,
        scratch_shapes=[
            pltpu.VMEM((NC, 256, CW), BF16),
            pltpu.VMEM((D, 768), BF16),
            pltpu.VMEM((512, D), BF16),
            pltpu.VMEM((16, PAGE, 2 * HD), BF16),
            pltpu.VMEM((2, SPAN, 2 * HD), BF16),
            pltpu.VMEM((256, 768), F32),
            pltpu.VMEM((512, 2 * HD), BF16),
            pltpu.VMEM((512, HD), BF16),
            pltpu.VMEM((4 * B_ROWS, HD), BF16),
            pltpu.VMEM((64, HD), BF16),
            pltpu.VMEM((2, 256, HD), F32),
            pltpu.VMEM((512, SPAN + 256), F32),
            pltpu.VMEM((4 * B_ROWS, SPAN + 384), F32),
            pltpu.VMEM((64, 2048), F32),
            pltpu.VMEM((512, SPAN + 256), BF16),
            pltpu.VMEM((4 * B_ROWS, SPAN + 384), BF16),
            pltpu.VMEM((64, 2048), BF16),
            pltpu.VMEM((512, HD), F32),
            pltpu.VMEM((4 * B_ROWS, HD), F32),
            pltpu.VMEM((16, 2048), F32),
            pltpu.VMEM((256, 512), BF16),
            pltpu.VMEM((NC, 2, 4, 32, CW), BF16),
            pltpu.VMEM((NC, 2, 16, CA), BF16),
            pltpu.VMEM((NC, 2, 16, CA), BF16),
            pltpu.VMEM((NC, 2, 32, CA), BF16),
            pltpu.VMEM((NC, 2, 32, CA), BF16),
            pltpu.VMEM((NC, 32, CA), BF16),
            pltpu.VMEM((NC, 4, 32, cb), BF16),
            pltpu.VMEM((NC, 16, cb), BF16),
            pltpu.VMEM((NC, 16, cb), BF16),
            pltpu.VMEM((NC, 32, cb), BF16),
            pltpu.VMEM((NC, 32, cb), BF16),
            dma((4,)),
            dma((2 + 2 * NC,)),
            dma((2 + 2 * NC,)),
            dma((NC, 17)),
            dma((NC, 17)),
            dma,
            dma,
            dma((NC, 10)),
            dma((NC, 10)),
        ],
        compiler_params=pltpu.CompilerParams(
            collective_id=0, has_side_effects=True, vmem_limit_bytes=60 * 1024 * 1024
        ),
    )(x, gain[None], freq, wq, wkv, wo, pool, table, offsets, lengths)


def solution(mesh):
    placed = (
        P(("req", "tensor"), None),
        P(),
        P(None, "tensor"),
        P(None, "tensor"),
        P("tensor", None),
        P(("req", "tensor"), None, None),
        P("req", None),
        P("req"),
        P("req"),
    )
    return jax.shard_map(
        shards, mesh=mesh, in_specs=placed, out_specs=P(("req", "tensor"), None), check_vma=False
    )
```

time: 441 us -> 95.4 us (0.22)
  waiting for transfers between devices: 210 us -> 0 us
  other arithmetic: 131 us -> 0 us
  Pallas kernels: 0 us -> 91.9 us
  matrix products: 41.2 us -> 0 us
  local copies, waits for them, and re-layouts: 38.4 us -> 3.23 us
  between operations: 13.8 us -> 0.01 us
    reduce_scatter x1 -> x0, waiting for transfers between devices: 153 us -> none  [shards(): lax.psum_scatter(jnp.dot(piece, output_weight, preferred_element_type=jnp...]
    and x52 -> x0, other arithmetic: 100 us -> none  [the longest x18 99.7 us: cached_block(): jnp.repeat(owned_page, page_len, total_repeat_length=key_span)]
    pallas_call x0 -> x1, Pallas kernels: none -> 91.9 us  [shards(): pl.pallas_call(kernel, name='block', out_shape=jax.ShapeDtypeStruct((32,...]
    all_gather x1 -> x0, waiting for transfers between devices: 55.6 us -> none  [shards(): project_piece = lax.all_gather(normed, 'tensor', axis=0, tiled=True)]
    dot_general x44 -> x0, matrix products: 41.2 us -> none  [the longest x1 10.3 us: shards(): jnp.dot(piece, output_weight, preferred_element_type=jnp.float32)]
    gather x35 -> x0, local copies, waits for them, and re-layouts: 24 us -> none  [the longest x18 12.5 us: cached_block(): fetched = jnp.take(pool_rows, local_page, axis=1)]
    dynamic_slice x16 -> x0, local copies, waits for them, and re-layouts: 9.91 us -> none  [cached_all(): lax.map(decode_one, (queries[2 * stretch_len:], page_table[2:], decode_le...]
    reduce_sum x20 -> x0, other arithmetic: 8.17 us -> none  [the longest x18 5.52 us: cached_block(): totals = jnp.sum(weights, axis=-1)]
  transfers between devices with their start and end apart: 7 -> 0, of which waited for: 3 -> 0; matrix products, arithmetic and copies ran while one was open for 8% -> 0% of each run, Pallas kernels for 0% -> 0%
where the time goes in v1:
time: 95.4 us; the launch traced here: 95.2 us
  Pallas kernels  91.9 us (96%)
  local copies, waits for them, and re-layouts  3.23 us (3%)
    pallas_call x1, Pallas kernels, shards(): pl.pallas_call(kernel, name='block', out_shape=jax.ShapeDtypeStruct((32,...  91.9 us
    unnamed x2, local copies, waits for them, and re-layouts  3.23 us

profile of v1, /device:TPU:160, one launch (start us, length us, event | category | flops | bytes accessed | tf_op | source)
XLA Modules:
  0.0 95.2 jit_solution(14462404739356607887)
XLA Ops:
  0.0 1.4 %copy.11.table_ref = s32[18,8]{1,0:T(8,128)} copy(s32[18,8]{0,1:T(8,128)} %param.16) | data formatting | bytes 1152 | tf_op args[6]
  1.4 91.9 %block.1 = bf16[32,8192]{1,0:T(8,128)(2,1)} custom-call(bf16[32,8192]{1,0:T(8,128)(2,1)} %x_ref.1, f32[1,8192]{1,0:T(1,128)} %bitcast.1, f32[1,128]{1,0:T(1,128)} %constant.7.freq_ref, bf16[8192,256]{1,0:T(8,128)(2,1)} %wq_hbm.1, bf16[8192,128]{1,0:T(8,128)(2,1)} %wkv_hbm.1, bf16[256,8192]{1,0:T(8,128)(2,1)} %wo_hbm.1, bf16[8,128,256]{2,1,0:T(8,128)(2,1)} %pool_hbm.1, ...), custom_call_target="tpu_custom_call" | custom-call | tf_op jit(solution)/shard_map/block/pallas_call | solution.py:450
  93.3 1.9 %copy.13 = bf16[32,8192]{1,0:T(8,128)(2,1)} copy(bf16[32,8192]{1,0:T(8,128)(2,1)} %block.1) | data formatting | bytes 1048576

commit v2 on v1

--- a/solution.py
+++ b/solution.py
@@ -29,11 +29,11 @@
 
 
 def kernel(
-    x_ref, gain_ref, freq_ref, wq_hbm, wkv_hbm, wo_hbm, pool_hbm, table_ref, off_ref, len_ref,
+    x_hbm, gain_ref, freq_ref, wq_hbm, wkv_hbm, wo_hbm, pool_hbm, table_hbm, off_ref, len_ref,
     out_ref,
-    xg, w, wo, pool, kvc, acc, newkv, qa, qb, qd, trig, sa, sb, sd, pa, pb, pd, la, lb, cnt, att,
+    x_ref, table_ref, xg, w, wo, pool, kvc, acc, newkv, qa, qb, qd, trig, sa, sb, sd, pa, pb, pd, la, lb, cnt, att,
     pbuf, r_al, r_ar, r_l, r_r, r_y, s_y, s_al, s_ar, s_l, s_r,
-    own_sem, ws_sem, wr_sem, ag_s, ag_r, kv_s, kv_r, rs_s, rs_r,
+    in_sem, own_sem, ws_sem, wr_sem, ag_s, ag_r, kv_s, kv_r, rs_s, rs_r,
 ):
     req = lax.axis_index("req")
     me = lax.axis_index("tensor")
@@ -49,6 +49,15 @@
         return pltpu.make_async_remote_copy(
             src_ref=src, dst_ref=dst, send_sem=ssem, recv_sem=rsem, device_id=to, device_id_type=MESH
         )
+
+    barrier = pltpu.get_barrier_semaphore()
+    for to in (core_dev, right, left, across):
+        pl.semaphore_signal(barrier, inc=1, device_id=to, device_id_type=MESH)
+
+    rows_in = pltpu.make_async_copy(x_hbm, x_ref, in_sem.at[0])
+    table_in = pltpu.make_async_copy(table_hbm, table_ref, in_sem.at[1])
+    rows_in.start()
+    table_in.start()
 
     qcol = pl.multiple_of(c * 256, 256)
     kcol = pl.multiple_of(512 + c * 128, 128)
@@ -63,12 +72,9 @@
     for copy in own:
         copy.start()
 
-    barrier = pltpu.get_barrier_semaphore()
-    for to in (core_dev, right, left, across):
-        pl.semaphore_signal(barrier, inc=1, device_id=to, device_id_type=MESH)
-
     mine = pl.multiple_of((h * 4 + x) * 32, 32)
     total = jnp.zeros((32, 1), F32)
+    rows_in.wait()
     for i in range(NC):
         v = x_ref[:, i * CW : (i + 1) * CW].astype(F32)
         total = total + jnp.sum(v * v, axis=1, keepdims=True)
@@ -140,9 +146,6 @@
 
     swap_pool.start()
     acc[...] = jnp.zeros_like(acc)
-    own[0].wait()
-    own[1].wait()
-    own[2].wait()
 
     def gather_step(s, carry):
         @pl.when(s < NC)
@@ -152,9 +155,9 @@
             swap_q(s).start()
             swap_kv(s).start()
 
-        @pl.when((s >= 1) & (s < NC + 1))
-        def _():
-            i = s - 1
+        @pl.when((s >= 2) & (s < NC + 2))
+        def _():
+            i = s - 2
             gather(0, i).wait_recv()
             gather(3, i).start()
             gather(4, i).start()
@@ -169,9 +172,9 @@
             gather(2, i).wait_recv()
             gather(6, i).start()
 
-        @pl.when((s >= 2) & (s < NC + 2))
-        def _():
-            i = s - 2
+        @pl.when((s >= 4) & (s < NC + 4))
+        def _():
+            i = s - 4
             gather(12, i).wait_recv()
             gather(13, i).wait_recv()
             gather(16, i).start()
@@ -180,13 +183,13 @@
             gather(4, i).wait_recv()
             gather(8, i).start()
 
-        @pl.when(s == 3)
+        @pl.when(s == 5)
         def _():
             prepare()
 
-        @pl.when(s >= 3)
-        def _():
-            i = s - 3
+        @pl.when(s >= 6)
+        def _():
+            i = s - 6
             for k in (5, 6, 7, 8, 11, 14, 15, 16):
                 gather(k, i).wait_recv()
             swap_q(i).wait_recv()
@@ -197,11 +200,15 @@
         return carry
 
     def prepare():
+        own[0].wait()
+        own[1].wait()
+        own[2].wait()
+        table_in.wait()
         swap_pool.wait_recv()
         swap_wo.start()
         for st in range(2):
             for j in range(MAXP):
-                kvc[st, j * PAGE : (j + 1) * PAGE, :] = pool[table_ref[st, j]]
+                kvc[st, j * PAGE : (j + 1) * PAGE, :] = pool[table_ref[j, st]]
         slot = lax.broadcasted_iota(jnp.int32, (16, 2048), 1)
         page, inside = slot // PAGE, slot % PAGE
         rid = lax.broadcasted_iota(jnp.int32, (16, 1), 0)
@@ -212,7 +219,7 @@
         for j in range(MAXP):
             named = jnp.zeros((16, 1), jnp.int32)
             for b in range(16):
-                named = jnp.where(rid == b, table_ref[2 + b, j], named)
+                named = jnp.where(rid == b, table_ref[j, 2 + b], named)
             seen = (page == named) & (inside + j * PAGE < length)
             count = count + jnp.where(seen, 1.0, 0.0)
         cnt[...] = count
@@ -226,7 +233,7 @@
         trig[0] = jnp.cos(angle)
         trig[1] = jnp.where(lane < HD // 2, -jnp.sin(angle), jnp.sin(angle))
 
-    lax.fori_loop(0, NC + 3, gather_step, 0)
+    lax.fori_loop(0, NC + 6, gather_step, 0)
 
     def rotated(col):
         v = acc[:, col : col + HD]
@@ -377,9 +384,9 @@
             for k in (0, 1, 5):
                 scatter(k, s).start()
 
-        @pl.when((s >= 1) & (s < NC + 1))
-        def _():
-            i = s - 1
+        @pl.when((s >= 2) & (s < NC + 2))
+        def _():
+            i = s - 2
             scatter(0, i).wait_recv()
             pbuf[i, :, xr, 0:16, 0:CA] = (f(pbuf[i, :, xr, 0:16, 0:CA]) + f(r_al[i])).astype(BF16)
             scatter(1, i).wait_recv()
@@ -391,9 +398,9 @@
             scatter(6, i).start()
             scatter(7, i).start()
 
-        @pl.when((s >= 2) & (s < NC + 2))
-        def _():
-            i = s - 2
+        @pl.when((s >= 4) & (s < NC + 4))
+        def _():
+            i = s - 4
             scatter(2, i).wait_recv()
             scatter(3, i).wait_recv()
             pbuf[i, 1 - h, x, :, 0:CA] = (
@@ -407,9 +414,9 @@
             scatter(8, i).start()
             scatter(9, i).start()
 
-        @pl.when(s >= 3)
-        def _():
-            i = s - 3
+        @pl.when(s >= 6)
+        def _():
+            i = s - 6
             scatter(4, i).wait_recv()
             ca = pl.ds(pl.multiple_of(i * CW, 128), CA)
             cb = pl.ds(pl.multiple_of(i * CW + CA, 128), CW - CA)
@@ -422,7 +429,7 @@
 
         return carry
 
-    lax.fori_loop(0, NC + 3, scatter_step, 0)
+    lax.fori_loop(0, NC + 6, scatter_step, 0)
 
     def drain(i, carry):
         for k in range(17):
@@ -451,9 +458,11 @@
         kernel,
         name="block",
         out_shape=jax.ShapeDtypeStruct((32, D), BF16),
-        in_specs=[vmem, vmem, vmem, anyw, anyw, anyw, anyw, smem, smem, smem],
+        in_specs=[anyw, vmem, vmem, anyw, anyw, anyw, anyw, anyw, smem, smem],
         out_specs=vmem,
         scratch_shapes=[
+            pltpu.VMEM((32, D), BF16),
+            pltpu.SMEM((MAXP, 18), jnp.int32),
             pltpu.VMEM((NC, 256, CW), BF16),
             pltpu.VMEM((D, 768), BF16),
             pltpu.VMEM((512, D), BF16),
@@ -486,6 +495,7 @@
             pltpu.VMEM((NC, 16, cb), BF16),
             pltpu.VMEM((NC, 32, cb), BF16),
             pltpu.VMEM((NC, 32, cb), BF16),
+            dma((2,)),
             dma((4,)),
             dma((2 + 2 * NC,)),
             dma((2 + 2 * NC,)),
@@ -499,7 +509,7 @@
         compiler_params=pltpu.CompilerParams(
             collective_id=0, has_side_effects=True, vmem_limit_bytes=60 * 1024 * 1024
         ),
-    )(x, gain[None], freq, wq, wkv, wo, pool, table, offsets, lengths)
+    )(x, gain[None], freq, wq, wkv, wo, pool, table.T, offsets, lengths)
 
 
 def solution(mesh):

time: 95.4 us -> 89 us (0.933); the launches traced: 95.2 us -> 87.5 us
  Pallas kernels: 91.9 us -> 85.6 us
  local copies, waits for them, and re-layouts: 3.23 us -> 1.87 us
    pallas_call x1, Pallas kernels: 91.9 us -> 85.6 us  [shards(): pl.pallas_call(kernel, name='block', out_shape=jax.ShapeDtypeStruct((32,...]
    unnamed x2 -> x1, local copies, waits for them, and re-layouts: 3.23 us -> 1.87 us
where the time goes in v2:
time: 89 us; the launch traced here: 87.5 us
  Pallas kernels  85.6 us (96%)
  local copies, waits for them, and re-layouts  1.87 us (2%)
    pallas_call x1, Pallas kernels, shards(): pl.pallas_call(kernel, name='block', out_shape=jax.ShapeDtypeStruct((32,...  85.6 us
    unnamed x1, local copies, waits for them, and re-layouts  1.87 us

profile of v2, /device:TPU:160, one launch (start us, length us, event | category | flops | bytes accessed | tf_op | source)
XLA Modules:
  0.0 87.5 jit_solution(8860212773217211708)
XLA Ops:
  0.0 85.6 %block.1 = bf16[32,8192]{1,0:T(8,128)(2,1)} custom-call(bf16[32,8192]{1,0:T(8,128)(2,1)} %x_hbm.1, f32[1,8192]{1,0:T(1,128)} %bitcast.2, f32[1,128]{1,0:T(1,128)} %constant.7.freq_ref, bf16[8192,256]{1,0:T(8,128)(2,1)} %wq_hbm.1, bf16[8192,128]{1,0:T(8,128)(2,1)} %wkv_hbm.1, bf16[256,8192]{1,0:T(8,128)(2,1)} %wo_hbm.1, bf16[8,128,256]{2,1,0:T(8,128)(2,1)} %pool_hbm.1, ...), custom_call_target="tpu_custom_call" | custom-call | tf_op jit(solution)/shard_map/block/pallas_call | solution.py:457
  85.6 1.9 %copy.12 = bf16[32,8192]{1,0:T(8,128)(2,1)} copy(bf16[32,8192]{1,0:T(8,128)(2,1)} %block.1) | data formatting | bytes 1048576

commit v3 on v2

v3 whole, which is shorter than its diff:
```python
import functools

import jax
import jax.numpy as jnp
import numpy as np
from jax import lax
from jax.experimental import pallas as pl
from jax.experimental.pallas import tpu as pltpu
from jax.sharding import PartitionSpec as P

HD = 128
C = 248
PAGE = 128
MAXP = 8
ROWS = 512
D = 8192
CW = 2048
NN = D // CW
NB = 2
NC = NB * NN
CA = 1152
AH = 640
BH = CA + 384
eps_norm = 1e-06
rope_base = 1000000.0
neg_big = -1e30
MESH = pl.DeviceIdType.MESH
F32 = jnp.float32
BF16 = jnp.bfloat16
B_LO = (64, 48)
SPAN = MAXP * PAGE


def kernel(
    x_hbm, gain_ref, freq_ref, wq_hbm, wkv_hbm, wo_hbm, pool_hbm, table_hbm, off_ref, len_ref,
    out_ref,
    x_ref, table_ref, xg, w, wo, pool, kvc, acc, newkv, qa, qb, qd, trig, sc_ref, sf_ref, sd, pc, pd,
    m_ref, l_ref, o_ref, cnt, att, pbuf, r_al, r_ar, r_l, r_r, r_y, s_y, s_al, s_ar, s_l, s_r,
    in_sem, own_sem, ws_sem, wr_sem, ag_s, ag_r, kv_s, kv_r, rs_s, rs_r,
):
    req = lax.axis_index("req")
    me = lax.axis_index("tensor")
    h, x, c = me // 8, (me // 2) % 4, me % 2

    def dev(hh, xx, cc):
        return (req, hh * 8 + xx * 2 + cc)

    xr, xl, xo = lax.rem(x + 1, 4), lax.rem(x + 3, 4), lax.rem(x + 2, 4)
    core_dev, right, left, across = dev(h, x, 1 - c), dev(h, xr, c), dev(h, xl, c), dev(1 - h, x, c)

    def send(src, dst, ssem, rsem, to):
        return pltpu.make_async_remote_copy(
            src_ref=src, dst_ref=dst, send_sem=ssem, recv_sem=rsem, device_id=to, device_id_type=MESH
        )

    barrier = pltpu.get_barrier_semaphore()
    for to in (core_dev, right, left, across):
        pl.semaphore_signal(barrier, inc=1, device_id=to, device_id_type=MESH)

    rows_in = pltpu.make_async_copy(x_hbm, x_ref, in_sem.at[0])
    table_in = pltpu.make_async_copy(table_hbm, table_ref, in_sem.at[1])
    rows_in.start()
    table_in.start()

    qcol = pl.multiple_of(c * 256, 256)
    kcol = pl.multiple_of(512 + c * 128, 128)
    orow = pl.multiple_of(c * 256, 256)
    prow = c * 8
    own = [
        pltpu.make_async_copy(pool_hbm, pool.at[pl.ds(prow, 8)], own_sem.at[0]),
        pltpu.make_async_copy(wq_hbm, w.at[:, pl.ds(qcol, 256)], own_sem.at[1]),
        pltpu.make_async_copy(wkv_hbm, w.at[:, pl.ds(kcol, 128)], own_sem.at[2]),
        pltpu.make_async_copy(wo_hbm, wo.at[pl.ds(orow, 256)], own_sem.at[3]),
    ]
    for copy in own:
        copy.start()

    mine = pl.multiple_of((h * 4 + x) * 16, 16)
    total = jnp.zeros((32, 1), F32)
    rows_in.wait()
    for i in range(NN):
        v = x_ref[:, i * CW : (i + 1) * CW].astype(F32)
        total = total + jnp.sum(v * v, axis=1, keepdims=True)
    inv = lax.rsqrt(total * (1.0 / D) + eps_norm)
    for i in range(NN):
        v = x_ref[:, i * CW : (i + 1) * CW].astype(F32)
        v = (v * inv * gain_ref[:, i * CW : (i + 1) * CW]).astype(BF16)
        for b in range(NB):
            xg[b * NN + i, pl.ds(mine, 16), :] = v[b * 16 : (b + 1) * 16]

    pl.semaphore_wait(barrier, 4)

    swap_pool = send(pool_hbm, pool.at[pl.ds(prow, 8)], ws_sem.at[0], wr_sem.at[0], core_dev)
    swap_wo = send(wo_hbm, wo.at[pl.ds(orow, 256)], ws_sem.at[1], wr_sem.at[1], core_dev)

    def swap_q(i):
        r = pl.ds(pl.multiple_of(i * CW, CW), CW)
        return send(wq_hbm.at[r], w.at[r, pl.ds(qcol, 256)], ws_sem.at[2 + i], wr_sem.at[2 + i], core_dev)

    def swap_kv(i):
        r = pl.ds(pl.multiple_of(i * CW, CW), CW)
        return send(
            wkv_hbm.at[r], w.at[r, pl.ds(kcol, 128)], ws_sem.at[2 + NN + i], wr_sem.at[2 + NN + i], core_dev
        )

    def block(hh, xx):
        return pl.multiple_of((hh * 4 + xx) * 16, 16)

    b_own, b_par = block(h, x), block(1 - h, x)
    b_l, b_r, b_o = block(h, xl), block(h, xr), block(h, xo)
    p_l, p_r = block(1 - h, xl), block(1 - h, xr)

    def gather(k, i):
        row, lo, hi, to = (
            (b_own, 0, CA, across),
            (b_own, 0, CA, right),
            (b_own, 0, CA, left),
            (b_par, 0, CA, right),
            (b_par, 0, CA, left),
            (b_l, 0, AH, right),
            (b_r, AH, CA, left),
            (p_l, 0, AH, right),
            (p_r, AH, CA, left),
            (b_own, CA, CW, right),
            (b_own, CA, CW, left),
            (b_own, CA, CW, across),
            (b_l, CA, BH, right),
            (b_r, BH, CW, left),
            (b_l, CA, CW, across),
            (b_r, CA, CW, across),
            (b_o, CA, CW, across),
        )[k]
        ref = xg.at[i, pl.ds(row, 16), lo:hi]
        return send(ref, ref, ag_s.at[i, k], ag_r.at[i, k], to)

    swap_pool.start()
    acc[...] = jnp.zeros_like(acc)

    def gather0(i):
        for k in (0, 1, 2, 9, 10, 11):
            gather(k, i).start()

    def gather1(i):
        gather(0, i).wait_recv()
        gather(3, i).start()
        gather(4, i).start()
        gather(9, i).wait_recv()
        gather(12, i).start()
        gather(14, i).start()
        gather(10, i).wait_recv()
        gather(13, i).start()
        gather(15, i).start()
        gather(1, i).wait_recv()
        gather(5, i).start()
        gather(2, i).wait_recv()
        gather(6, i).start()

    def gather2(i):
        gather(12, i).wait_recv()
        gather(13, i).wait_recv()
        gather(16, i).start()
        gather(3, i).wait_recv()
        gather(7, i).start()
        gather(4, i).wait_recv()
        gather(8, i).start()

    def project(b, n):
        i = b * NN + n
        for k in (5, 6, 7, 8, 11, 14, 15, 16):
            gather(k, i).wait_recv()
        r = pl.ds(pl.multiple_of(n * CW, CW), CW)
        acc[b] += jnp.dot(xg[i], w[r, :], preferred_element_type=F32)

    def gather_step(s, carry):
        @pl.when(s < NC)
        def _():
            gather0(s)

        @pl.when(s < NN)
        def _():
            swap_q(s).start()
            swap_kv(s).start()

        @pl.when(s >= 2)
        def _():
            gather1(s - 2)

        @pl.when(s >= 4)
        def _():
            gather2(s - 4)

        @pl.when(s == 4)
        def _():
            prepare()

        @pl.when(s >= 5)
        def _():
            n = s - 5
            swap_q(n).wait_recv()
            swap_kv(n).wait_recv()
            project(0, n)

        return carry

    def prepare():
        own[0].wait()
        own[1].wait()
        own[2].wait()
        table_in.wait()
        swap_pool.wait_recv()
        swap_wo.start()
        for st in range(2):
            for j in range(MAXP):
                kvc[st, j * PAGE : (j + 1) * PAGE, :] = pool[table_ref[j, st]]
        slot = lax.broadcasted_iota(jnp.int32, (16, 2048), 1)
        page, inside = slot // PAGE, slot % PAGE
        rid = lax.broadcasted_iota(jnp.int32, (16, 1), 0)
        length = jnp.zeros((16, 1), jnp.int32)
        for b in range(16):
            length = jnp.where(rid == b, len_ref[b], length)
        count = jnp.zeros((16, 2048), F32)
        for j in range(MAXP):
            named = jnp.zeros((16, 1), jnp.int32)
            for b in range(16):
                named = jnp.where(rid == b, table_ref[j, 2 + b], named)
            seen = (page == named) & (inside + j * PAGE < length)
            count = count + jnp.where(seen, 1.0, 0.0)
        cnt[...] = count
        for b in range(NB):
            g = row_globals(b, lax.broadcasted_iota(jnp.int32, (128, 1), 0))
            position = jnp.where(g < C, off_ref[0] + g, off_ref[1] + g - C)
            for d in range(16):
                position = jnp.where(g == 2 * C + d, len_ref[d], position)
            angle = position.astype(F32) * freq_ref[...]
            lane = lax.broadcasted_iota(jnp.int32, (128, HD), 1)
            trig[0, b] = jnp.cos(angle)
            trig[1, b] = jnp.where(lane < HD // 2, -jnp.sin(angle), jnp.sin(angle))

    def row_globals(b, lr):
        return ((lr // 16) * 2 + c) * 32 + b * 16 + lr % 16

    def key_globals(row):
        j = row // 256 * 4 + row % 64 // 16
        return (j * 2 + row // 128 % 2) * 32 + row // 64 % 2 * 16 + row % 16

    def rotated(b, col):
        v = acc[b, :, col : col + HD]
        return (v * trig[0, b] + pltpu.roll(v, HD // 2, 1) * trig[1, b]).astype(BF16)

    def swap_new(b, half):
        ref = newkv.at[pl.ds(pl.multiple_of(half * 256 + c * 128 + b * 64, 64), 64)]
        return send(ref, ref, kv_s.at[b, half], kv_r.at[b, half], core_dev)

    def head_rows(b, n):
        lo = B_LO[b]
        return slice(n * (128 - lo), (n + 1) * (128 - lo))

    def place(b):
        k = rotated(b, 512)
        v = acc[b, :, 640:768].astype(BF16)
        for half in range(2):
            rows = pl.ds(pl.multiple_of(half * 256 + c * 128 + b * 64, 64), 64)
            newkv[rows, 0:HD] = k[half * 64 : (half + 1) * 64]
            newkv[rows, HD : 2 * HD] = v[half * 64 : (half + 1) * 64]
        for n in range(4):
            q = rotated(b, n * HD)
            qa[b, n * 64 : (n + 1) * 64, :] = q[0:64]
            qb[b, head_rows(b, n), :] = q[B_LO[b] : 128]
            if b == 1:
                qd[n * 16 : (n + 1) * 16, :] = q[112:128]
            if n == 0:
                swap_new(b, 0).start()
                swap_new(b, 1).start()

    def nt(a, b):
        return lax.dot_general(a, b, (((1,), (1,)), ((), ())), preferred_element_type=F32)

    scale = HD ** (-0.5)

    def queries(b, st):
        return qa[b] if st == 0 else qb[b, 0 : 4 * (128 - B_LO[b]), :]

    def cached(b, st):
        q = queries(b, st)
        n = q.shape[0]
        sc_ref[0:n, :] = nt(q, kvc[st, :, 0:HD])
        slots = lax.broadcasted_iota(jnp.int32, (1, SPAN), 1)
        limit = off_ref[st]

        def some(k, carry):
            rows = pl.ds(pl.multiple_of(k * 32, 32), 32)
            v = jnp.where(slots < limit, sc_ref[rows, :], neg_big)
            m = jnp.max(v, axis=1, keepdims=True)
            e = jnp.exp((v - m) * scale)
            m_ref[b, st, rows, :] = jnp.broadcast_to(m, (32, HD))
            l_ref[b, st, rows, :] = jnp.broadcast_to(jnp.sum(e, axis=1, keepdims=True), (32, HD))
            pc[rows, :] = e.astype(BF16)
            return carry

        lax.fori_loop(0, n // 32, some, 0, unroll=2)
        o_ref[b, st, 0:n, :] = jnp.dot(pc[0:n, :], kvc[st, :, HD : 2 * HD], preferred_element_type=F32)

    def fresh(b, st):
        q = queries(b, st)
        k0, width = (0, 256) if st == 0 else (128, 384)
        n = q.shape[0] // 4
        sf_ref[0 : 4 * n, 0:width] = nt(q, newkv[k0 : k0 + width, 0:HD])
        lo = 0 if st == 0 else B_LO[b]
        kg = key_globals(k0 + lax.broadcasted_iota(jnp.int32, (1, width), 1))
        qg = row_globals(b, lo + lax.broadcasted_iota(jnp.int32, (n, 1), 0))
        seen = (kg <= qg) & (kg < C if st == 0 else kg >= C)
        for head in range(4):
            rows = slice(head * n, (head + 1) * n)
            v = jnp.where(seen, sf_ref[rows, 0:width], neg_big)
            m1 = m_ref[b, st, rows, :]
            m = jnp.maximum(m1, jnp.max(v, axis=1, keepdims=True))
            alpha = jnp.exp((m1 - m) * scale)
            e = jnp.exp((v - m[:, 0:1]) * scale)
            tot = alpha * l_ref[b, st, rows, :] + jnp.sum(e, axis=1, keepdims=True)
            o = jnp.dot(e.astype(BF16), newkv[k0 : k0 + width, HD : 2 * HD], preferred_element_type=F32)
            o = ((alpha * o_ref[b, st, rows, :] + o) / tot).astype(BF16)
            cols = slice(head * HD, (head + 1) * HD)
            if st == 0:
                att[b, 0:64, cols] = o
            elif b == 0:
                att[b, 64:128, cols] = o
            else:
                near = lax.broadcasted_iota(jnp.int32, (16, 1), 0) >= 8 + 8 * (1 - c)
                att[b, 64:128, cols] = o[16:]
                att[b, 48:64, cols] = jnp.where(
                    near, o[0:16].astype(F32), att[b, 48:64, cols].astype(F32)
                ).astype(BF16)

    def decodes():
        for b in range(16):
            sd[:, b * 128 : (b + 1) * 128] = nt(qd[...], pool[b, :, 0:HD])
        self_s = nt(qd[...], newkv[496:512, 0:HD])
        kid = lax.broadcasted_iota(jnp.int32, (64, 16), 1)
        qid = lax.broadcasted_iota(jnp.int32, (64, 16), 0) % 16
        self_s = jnp.where(kid == qid, self_s, neg_big)
        for n in range(4):
            rows = slice(n * 16, (n + 1) * 16)
            own_s = self_s[n * 16 : (n + 1) * 16]
            count = cnt[...]
            v = jnp.where(count > 0.0, sd[rows, :], neg_big)
            m = jnp.maximum(jnp.max(v, axis=1, keepdims=True), jnp.max(own_s, axis=1, keepdims=True))
            e = count * jnp.exp((v - m) * scale)
            e_own = jnp.exp((own_s - m) * scale)
            tot = jnp.sum(e, axis=1, keepdims=True) + jnp.sum(e_own, axis=1, keepdims=True)
            pd[rows, :] = e.astype(BF16)
            o = jnp.dot(e_own.astype(BF16), newkv[496:512, HD : 2 * HD], preferred_element_type=F32)
            for b in range(16):
                o = o + jnp.dot(
                    pd[rows, b * 128 : (b + 1) * 128], pool[b, :, HD : 2 * HD], preferred_element_type=F32
                )
            att[1, 112:128, n * HD : (n + 1) * HD] = (o / tot).astype(BF16)

    lax.fori_loop(0, NC + 1, gather_step, 0)
    place(0)
    gather1(7)
    gather2(5)
    project(1, 0)
    cached(0, 0)
    gather2(6)
    project(1, 1)
    cached(0, 1)
    gather2(7)
    project(1, 2)
    project(1, 3)
    place(1)
    cached(1, 0)
    for b in range(NB):
        swap_new(b, 0).wait_recv()
        swap_new(b, 1).wait_recv()
    fresh(0, 0)
    fresh(0, 1)
    own[3].wait()
    swap_wo.wait_recv()

    def scatter(k, i):
        ss, rr = rs_s.at[i, k], rs_r.at[i, k]
        if k == 0:
            return send(pbuf.at[i, :, xo, :, 0:AH], r_al.at[i], ss, rr, right)
        if k == 1:
            return send(pbuf.at[i, :, xo, :, AH:CA], r_ar.at[i], ss, rr, left)
        if k == 2:
            return send(pbuf.at[i, :, xr, :, 0:CA], r_l.at[i], ss, rr, right)
        if k == 3:
            return send(pbuf.at[i, :, xl, :, 0:CA], r_r.at[i], ss, rr, left)
        if k == 4:
            return send(pbuf.at[i, 1 - h, x, :, 0:CA], r_y.at[i], ss, rr, across)
        if k == 5:
            return send(pbuf.at[i, 1 - h, :, :, CA:CW], s_y.at[i], ss, rr, across)
        if k == 6:
            return send(pbuf.at[i, h, xo, :, CA:BH], s_al.at[i], ss, rr, right)
        if k == 7:
            return send(pbuf.at[i, h, xo, :, BH:CW], s_ar.at[i], ss, rr, left)
        if k == 8:
            return send(pbuf.at[i, h, xr, :, CA:CW], s_l.at[i], ss, rr, right)
        return send(pbuf.at[i, h, xl, :, CA:CW], s_r.at[i], ss, rr, left)

    def f(v):
        return v.astype(F32)

    def scatter0(b, n):
        i = b * NN + n
        for k in range(CW // 256):
            col = pl.multiple_of(n * CW + k * 256, 256)
            prod = jnp.dot(att[b], wo[:, pl.ds(col, 256)], preferred_element_type=F32)
            pbuf[i, :, :, :, k * 256 : (k + 1) * 256] = prod.astype(BF16).reshape(2, 4, 16, 256)
        for k in (0, 1, 5):
            scatter(k, i).start()

    def scatter1(i):
        scatter(0, i).wait_recv()
        pbuf[i, :, xr, :, 0:AH] = (f(pbuf[i, :, xr, :, 0:AH]) + f(r_al[i])).astype(BF16)
        scatter(1, i).wait_recv()
        pbuf[i, :, xl, :, AH:CA] = (f(pbuf[i, :, xl, :, AH:CA]) + f(r_ar[i])).astype(BF16)
        scatter(2, i).start()
        scatter(3, i).start()
        scatter(5, i).wait_recv()
        pbuf[i, h, :, :, CA:CW] = (f(pbuf[i, h, :, :, CA:CW]) + f(s_y[i])).astype(BF16)
        scatter(6, i).start()
        scatter(7, i).start()

    def scatter2(i):
        scatter(2, i).wait_recv()
        scatter(3, i).wait_recv()
        pbuf[i, 1 - h, x, :, 0:CA] = (
            f(pbuf[i, 1 - h, x, :, 0:CA]) + f(r_l[i, 1 - h]) + f(r_r[i, 1 - h])
        ).astype(BF16)
        scatter(4, i).start()
        scatter(6, i).wait_recv()
        pbuf[i, h, xr, :, CA:BH] = (f(pbuf[i, h, xr, :, CA:BH]) + f(s_al[i])).astype(BF16)
        scatter(7, i).wait_recv()
        pbuf[i, h, xl, :, BH:CW] = (f(pbuf[i, h, xl, :, BH:CW]) + f(s_ar[i])).astype(BF16)
        scatter(8, i).start()
        scatter(9, i).start()

    def scatter3(b, n):
        i = b * NN + n
        scatter(4, i).wait_recv()
        rows = pl.ds(pl.multiple_of(b * 16, 16), 16)
        ca = pl.ds(pl.multiple_of(n * CW, 128), CA)
        cb = pl.ds(pl.multiple_of(n * CW + CA, 128), CW - CA)
        out_ref[rows, ca] = (
            f(pbuf[i, h, x, :, 0:CA]) + f(r_l[i, h]) + f(r_r[i, h]) + f(r_y[i])
        ).astype(BF16)
        scatter(8, i).wait_recv()
        scatter(9, i).wait_recv()
        out_ref[rows, cb] = (f(pbuf[i, h, x, :, CA:CW]) + f(s_l[i]) + f(s_r[i])).astype(BF16)

    def first_step(s, carry):
        scatter0(0, s)
        return carry

    lax.fori_loop(0, NN, first_step, 0)
    cached(1, 1)
    scatter1(0)
    fresh(1, 0)
    scatter1(1)
    fresh(1, 1)
    scatter1(2)
    scatter2(0)

    @pl.when(c == 1)
    def _():
        decodes()

    scatter1(3)
    scatter2(1)

    def second_step(s, carry):
        @pl.when(s < NN)
        def _():
            scatter0(1, s)

        @pl.when(s < 2)
        def _():
            scatter2(s + 2)

        @pl.when((s >= 2) & (s < 6))
        def _():
            scatter1(s + 2)

        @pl.when((s >= 4) & (s < 8))
        def _():
            scatter2(s)

        @pl.when(s < 4)
        def _():
            scatter3(0, s)

        @pl.when(s >= 6)
        def _():
            scatter3(1, s - 6)

        return carry

    lax.fori_loop(0, 10, second_step, 0)

    def drain(i, carry):
        for k in range(17):
            gather(k, i).wait_send()
        for k in range(10):
            scatter(k, i).wait_send()
        return carry

    lax.fori_loop(0, NC, drain, 0)
    swap_pool.wait_send()
    swap_wo.wait_send()
    for i in range(NN):
        swap_q(i).wait_send()
        swap_kv(i).wait_send()
    for b in range(NB):
        swap_new(b, 0).wait_send()
        swap_new(b, 1).wait_send()


def shards(x, gain, wq, wkv, wo, pool, table, offsets, lengths):
    half = np.arange(HD) % (HD // 2)
    freq = jnp.asarray((rope_base ** (-2.0 * half / HD)).astype(np.float32))[None]
    vmem = pl.BlockSpec(memory_space=pltpu.VMEM)
    smem = pl.BlockSpec(memory_space=pltpu.SMEM)
    anyw = pl.BlockSpec(memory_space=pl.ANY)
    cb = CW - CA
    dma = pltpu.SemaphoreType.DMA
    return pl.pallas_call(
        kernel,
        name="block",
        out_shape=jax.ShapeDtypeStruct((32, D), BF16),
        in_specs=[anyw, vmem, vmem, anyw, anyw, anyw, anyw, anyw, smem, smem],
        out_specs=vmem,
        scratch_shapes=[
            pltpu.VMEM((32, D), BF16),
            pltpu.SMEM((MAXP, 18), jnp.int32),
            pltpu.VMEM((NC, 128, CW), BF16),
            pltpu.VMEM((D, 768), BF16),
            pltpu.VMEM((512, D), BF16),
            pltpu.VMEM((16, PAGE, 2 * HD), BF16),
            pltpu.VMEM((2, SPAN, 2 * HD), BF16),
            pltpu.VMEM((NB, 128, 768), F32),
            pltpu.VMEM((512, 2 * HD), BF16),
            pltpu.VMEM((NB, 256, HD), BF16),
            pltpu.VMEM((NB, 320, HD), BF16),
            pltpu.VMEM((64, HD), BF16),
            pltpu.VMEM((2, NB, 128, HD), F32),
            pltpu.VMEM((320, SPAN), F32),
            pltpu.VMEM((320, 384), F32),
            pltpu.VMEM((64, 2048), F32),
            pltpu.VMEM((320, SPAN), BF16),
            pltpu.VMEM((64, 2048), BF16),
            pltpu.VMEM((NB, 2, 320, HD), F32),
            pltpu.VMEM((NB, 2, 320, HD), F32),
            pltpu.VMEM((NB, 2, 320, HD), F32),
            pltpu.VMEM((16, 2048), F32),
            pltpu.VMEM((NB, 128, 512), BF16),
            pltpu.VMEM((NC, 2, 4, 16, CW), BF16),
            pltpu.VMEM((NC, 2, 16, AH), BF16),
            pltpu.VMEM((NC, 2, 16, CA - AH), BF16),
            pltpu.VMEM((NC, 2, 16, CA), BF16),
            pltpu.VMEM((NC, 2, 16, CA), BF16),
            pltpu.VMEM((NC, 16, CA), BF16),
            pltpu.VMEM((NC, 4, 16, cb), BF16),
            pltpu.VMEM((NC, 16, BH - CA), BF16),
            pltpu.VMEM((NC, 16, CW - BH), BF16),
            pltpu.VMEM((NC, 16, cb), BF16),
            pltpu.VMEM((NC, 16, cb), BF16),
            dma((2,)),
            dma((4,)),
            dma((2 + 2 * NN,)),
            dma((2 + 2 * NN,)),
            dma((NC, 17)),
            dma((NC, 17)),
            dma((NB, 2)),
            dma((NB, 2)),
            dma((NC, 10)),
            dma((NC, 10)),
        ],
        compiler_params=pltpu.CompilerParams(
            collective_id=0, has_side_effects=True, vmem_limit_bytes=60 * 1024 * 1024
        ),
    )(x, gain[None], freq, wq, wkv, wo, pool, table.T, offsets, lengths)


def solution(mesh):
    placed = (
        P(("req", "tensor"), None),
        P(),
        P(None, "tensor"),
        P(None, "tensor"),
        P("tensor", None),
        P(("req", "tensor"), None, None),
        P("req", None),
        P("req"),
        P("req"),
    )
    return jax.shard_map(
        shards, mesh=mesh, in_specs=placed, out_specs=P(("req", "tensor"), None), check_vma=False
    )
```

time: 89 us -> 86.3 us (0.970); the launches traced: 87.5 us -> 86 us
  Pallas kernels: 85.6 us -> 84.1 us
    pallas_call x1, Pallas kernels: 85.6 us -> 84.1 us  [shards(): pl.pallas_call(kernel, name='block', out_shape=jax.ShapeDtypeStruct((32,...]
where the time goes in v3:
time: 86.3 us; the launch traced here: 86 us
  Pallas kernels  84.1 us (97%)
  local copies, waits for them, and re-layouts  1.87 us (2%)
    pallas_call x1, Pallas kernels, shards(): pl.pallas_call(kernel, name='block', out_shape=jax.ShapeDtypeStruct((32,...  84.1 us
    unnamed x1, local copies, waits for them, and re-layouts  1.87 us

profile of v3, /device:TPU:160, one launch (start us, length us, event | category | flops | bytes accessed | tf_op | source)
XLA Modules:
  0.0 86.0 jit_solution(9870164531279585093)
XLA Ops:
  0.0 84.1 %block.1 = bf16[32,8192]{1,0:T(8,128)(2,1)} custom-call(bf16[32,8192]{1,0:T(8,128)(2,1)} %x_hbm.1, f32[1,8192]{1,0:T(1,128)} %bitcast.2, f32[1,128]{1,0:T(1,128)} %constant.7.freq_ref, bf16[8192,256]{1,0:T(8,128)(2,1)} %wq_hbm.1, bf16[8192,128]{1,0:T(8,128)(2,1)} %wkv_hbm.1, bf16[256,8192]{1,0:T(8,128)(2,1)} %wo_hbm.1, bf16[8,128,256]{2,1,0:T(8,128)(2,1)} %pool_hbm.1, ...), custom_call_target="tpu_custom_call" | custom-call | tf_op jit(solution)/shard_map/block/pallas_call | solution.py:528
  84.2 1.9 %copy.12 = bf16[32,8192]{1,0:T(8,128)(2,1)} copy(bf16[32,8192]{1,0:T(8,128)(2,1)} %block.1) | data formatting | bytes 1048576

commit v4 on v3

--- a/solution.py
+++ b/solution.py
@@ -32,11 +32,11 @@
 
 
 def kernel(
-    x_hbm, gain_ref, freq_ref, wq_hbm, wkv_hbm, wo_hbm, pool_hbm, table_hbm, off_ref, len_ref,
-    out_ref,
-    x_ref, table_ref, xg, w, wo, pool, kvc, acc, newkv, qa, qb, qd, trig, sc_ref, sf_ref, sd, pc, pd,
+    x_hbm, gain_hbm, freq_hbm, wq_hbm, wkv_hbm, wo_hbm, pool_hbm, table_hbm, off_hbm, len_hbm,
+    out_hbm,
+    out_ref, x_ref, gain_ref, freq_ref, table_ref, off_ref, len_ref, xg, w, wo, pool, kvc, acc, newkv, qa, qb, qd, trig, sc_ref, sf_ref, sd, pc, pd,
     m_ref, l_ref, o_ref, cnt, att, pbuf, r_al, r_ar, r_l, r_r, r_y, s_y, s_al, s_ar, s_l, s_r,
-    in_sem, own_sem, ws_sem, wr_sem, ag_s, ag_r, kv_s, kv_r, rs_s, rs_r,
+    in_sem, out_sem, own_sem, ws_sem, wr_sem, ag_s, ag_r, kv_s, kv_r, rs_s, rs_r,
 ):
     req = lax.axis_index("req")
     me = lax.axis_index("tensor")
@@ -57,10 +57,21 @@
     for to in (core_dev, right, left, across):
         pl.semaphore_signal(barrier, inc=1, device_id=to, device_id_type=MESH)
 
-    rows_in = pltpu.make_async_copy(x_hbm, x_ref, in_sem.at[0])
-    table_in = pltpu.make_async_copy(table_hbm, table_ref, in_sem.at[1])
-    rows_in.start()
-    table_in.start()
+    inputs = [
+        pltpu.make_async_copy(src, dst, in_sem.at[k])
+        for k, (src, dst) in enumerate(
+            (
+                (x_hbm, x_ref),
+                (gain_hbm, gain_ref),
+                (freq_hbm, freq_ref),
+                (table_hbm, table_ref),
+                (off_hbm, off_ref),
+                (len_hbm, len_ref),
+            )
+        )
+    ]
+    for copy in inputs:
+        copy.start()
 
     qcol = pl.multiple_of(c * 256, 256)
     kcol = pl.multiple_of(512 + c * 128, 128)
@@ -72,12 +83,12 @@
         pltpu.make_async_copy(wkv_hbm, w.at[:, pl.ds(kcol, 128)], own_sem.at[2]),
         pltpu.make_async_copy(wo_hbm, wo.at[pl.ds(orow, 256)], own_sem.at[3]),
     ]
+    mine = pl.multiple_of((h * 4 + x) * 16, 16)
+    total = jnp.zeros((32, 1), F32)
+    inputs[0].wait()
+    inputs[1].wait()
     for copy in own:
         copy.start()
-
-    mine = pl.multiple_of((h * 4 + x) * 16, 16)
-    total = jnp.zeros((32, 1), F32)
-    rows_in.wait()
     for i in range(NN):
         v = x_ref[:, i * CW : (i + 1) * CW].astype(F32)
         total = total + jnp.sum(v * v, axis=1, keepdims=True)
@@ -164,12 +175,13 @@
         gather(4, i).wait_recv()
         gather(8, i).start()
 
-    def project(b, n):
-        i = b * NN + n
+    def arrived(i):
         for k in (5, 6, 7, 8, 11, 14, 15, 16):
             gather(k, i).wait_recv()
+
+    def project(b, n, lo=0, hi=768):
         r = pl.ds(pl.multiple_of(n * CW, CW), CW)
-        acc[b] += jnp.dot(xg[i], w[r, :], preferred_element_type=F32)
+        acc[b, :, lo:hi] += jnp.dot(xg[b * NN + n], w[r, lo:hi], preferred_element_type=F32)
 
     def gather_step(s, carry):
         @pl.when(s < NC)
@@ -198,6 +210,7 @@
             n = s - 5
             swap_q(n).wait_recv()
             swap_kv(n).wait_recv()
+            arrived(n)
             project(0, n)
 
         return carry
@@ -206,7 +219,8 @@
         own[0].wait()
         own[1].wait()
         own[2].wait()
-        table_in.wait()
+        for copy in inputs[2:]:
+            copy.wait()
         swap_pool.wait_recv()
         swap_wo.start()
         for st in range(2):
@@ -255,22 +269,25 @@
         lo = B_LO[b]
         return slice(n * (128 - lo), (n + 1) * (128 - lo))
 
-    def place(b):
+    def place_new(b):
         k = rotated(b, 512)
         v = acc[b, :, 640:768].astype(BF16)
         for half in range(2):
             rows = pl.ds(pl.multiple_of(half * 256 + c * 128 + b * 64, 64), 64)
             newkv[rows, 0:HD] = k[half * 64 : (half + 1) * 64]
             newkv[rows, HD : 2 * HD] = v[half * 64 : (half + 1) * 64]
+
+    def place_queries(b):
         for n in range(4):
             q = rotated(b, n * HD)
             qa[b, n * 64 : (n + 1) * 64, :] = q[0:64]
             qb[b, head_rows(b, n), :] = q[B_LO[b] : 128]
             if b == 1:
                 qd[n * 16 : (n + 1) * 16, :] = q[112:128]
-            if n == 0:
-                swap_new(b, 0).start()
-                swap_new(b, 1).start()
+
+    def exchange(b):
+        swap_new(b, 0).start()
+        swap_new(b, 1).start()
 
     def nt(a, b):
         return lax.dot_general(a, b, (((1,), (1,)), ((), ())), preferred_element_type=F32)
@@ -356,19 +373,28 @@
             att[1, 112:128, n * HD : (n + 1) * HD] = (o / tot).astype(BF16)
 
     lax.fori_loop(0, NC + 1, gather_step, 0)
-    place(0)
     gather1(7)
     gather2(5)
-    project(1, 0)
+    place_new(0)
+    place_queries(0)
+    exchange(0)
     cached(0, 0)
     gather2(6)
-    project(1, 1)
     cached(0, 1)
     gather2(7)
+    arrived(4)
+    project(1, 0)
+    arrived(5)
+    project(1, 1)
+    arrived(6)
     project(1, 2)
-    project(1, 3)
-    place(1)
-    cached(1, 0)
+    arrived(7)
+    project(1, 3, 512, 768)
+    place_new(1)
+    project(1, 3, 0, 256)
+    exchange(1)
+    project(1, 3, 256, 512)
+    place_queries(1)
     for b in range(NB):
         swap_new(b, 0).wait_recv()
         swap_new(b, 1).wait_recv()
@@ -450,15 +476,21 @@
         scatter(9, i).wait_recv()
         out_ref[rows, cb] = (f(pbuf[i, h, x, :, CA:CW]) + f(s_l[i]) + f(s_r[i])).astype(BF16)
 
+    def written(b, n):
+        rows = pl.ds(pl.multiple_of(b * 16, 16), 16)
+        cols = pl.ds(pl.multiple_of(n * CW, 128), CW)
+        return pltpu.make_async_copy(out_ref.at[rows, cols], out_hbm.at[rows, cols], out_sem.at[b * NN + n])
+
     def first_step(s, carry):
         scatter0(0, s)
         return carry
 
     lax.fori_loop(0, NN, first_step, 0)
+    cached(1, 0)
+    scatter1(0)
     cached(1, 1)
-    scatter1(0)
+    scatter1(1)
     fresh(1, 0)
-    scatter1(1)
     fresh(1, 1)
     scatter1(2)
     scatter2(0)
@@ -490,10 +522,12 @@
         @pl.when(s < 4)
         def _():
             scatter3(0, s)
+            written(0, s).start()
 
         @pl.when(s >= 6)
         def _():
             scatter3(1, s - 6)
+            written(1, s - 6).start()
 
         return carry
 
@@ -510,6 +544,8 @@
     swap_pool.wait_send()
     swap_wo.wait_send()
     for i in range(NN):
+        for b in range(NB):
+            written(b, i).wait()
         swap_q(i).wait_send()
         swap_kv(i).wait_send()
     for b in range(NB):
@@ -520,8 +556,6 @@
 def shards(x, gain, wq, wkv, wo, pool, table, offsets, lengths):
     half = np.arange(HD) % (HD // 2)
     freq = jnp.asarray((rope_base ** (-2.0 * half / HD)).astype(np.float32))[None]
-    vmem = pl.BlockSpec(memory_space=pltpu.VMEM)
-    smem = pl.BlockSpec(memory_space=pltpu.SMEM)
     anyw = pl.BlockSpec(memory_space=pl.ANY)
     cb = CW - CA
     dma = pltpu.SemaphoreType.DMA
@@ -529,11 +563,16 @@
         kernel,
         name="block",
         out_shape=jax.ShapeDtypeStruct((32, D), BF16),
-        in_specs=[anyw, vmem, vmem, anyw, anyw, anyw, anyw, anyw, smem, smem],
-        out_specs=vmem,
+        in_specs=[anyw] * 10,
+        out_specs=anyw,
         scratch_shapes=[
             pltpu.VMEM((32, D), BF16),
+            pltpu.VMEM((32, D), BF16),
+            pltpu.VMEM((1, D), F32),
+            pltpu.VMEM((1, HD), F32),
             pltpu.SMEM((MAXP, 18), jnp.int32),
+            pltpu.SMEM((2,), jnp.int32),
+            pltpu.SMEM((16,), jnp.int32),
             pltpu.VMEM((NC, 128, CW), BF16),
             pltpu.VMEM((D, 768), BF16),
             pltpu.VMEM((512, D), BF16),
@@ -566,7 +605,8 @@
             pltpu.VMEM((NC, 16, CW - BH), BF16),
             pltpu.VMEM((NC, 16, cb), BF16),
             pltpu.VMEM((NC, 16, cb), BF16),
-            dma((2,)),
+            dma((6,)),
+            dma((NC,)),
             dma((4,)),
             dma((2 + 2 * NN,)),
             dma((2 + 2 * NN,)),

time: 86.3 us -> 81.8 us (0.948)
  Pallas kernels: 84.1 us -> 79.8 us
    pallas_call x1, Pallas kernels: 84.1 us -> 79.8 us  [shards(): pl.pallas_call(kernel, name='block', out_shape=jax.ShapeDtypeStruct((32,...]
where the time goes in v4:
time: 81.8 us; the launch traced here: 81.7 us
  Pallas kernels  79.8 us (98%)
  local copies, waits for them, and re-layouts  1.87 us (2%)
    pallas_call x1, Pallas kernels, shards(): pl.pallas_call(kernel, name='block', out_shape=jax.ShapeDtypeStruct((32,...  79.8 us
    unnamed x1, local copies, waits for them, and re-layouts  1.87 us

profile of v4, /device:TPU:160, one launch (start us, length us, event | category | flops | bytes accessed | tf_op | source)
XLA Modules:
  0.0 81.7 jit_solution(2936372650914823026)
XLA Ops:
  0.0 79.8 %block.1 = bf16[32,8192]{1,0:T(8,128)(2,1)} custom-call(bf16[32,8192]{1,0:T(8,128)(2,1)} %x_hbm.1, f32[1,8192]{1,0:T(1,128)} %bitcast.2, f32[1,128]{1,0:T(1,128)} %constant.7.freq_hbm, bf16[8192,256]{1,0:T(8,128)(2,1)} %wq_hbm.1, bf16[8192,128]{1,0:T(8,128)(2,1)} %wkv_hbm.1, bf16[256,8192]{1,0:T(8,128)(2,1)} %wo_hbm.1, bf16[8,128,256]{2,1,0:T(8,128)(2,1)} %pool_hbm.1, ...), custom_call_target="tpu_custom_call" | custom-call | tf_op jit(solution)/shard_map/block/pallas_call | solution.py:562
  79.8 1.9 %copy.12 = bf16[32,8192]{1,0:T(8,128)(2,1)} copy(bf16[32,8192]{1,0:T(8,128)(2,1)} %block.1) | data formatting | bytes 1048576

commit v5 on v4

--- a/solution.py
+++ b/solution.py
@@ -487,51 +487,39 @@
 
     lax.fori_loop(0, NN, first_step, 0)
     cached(1, 0)
-    scatter1(0)
     cached(1, 1)
-    scatter1(1)
     fresh(1, 0)
     fresh(1, 1)
-    scatter1(2)
-    scatter2(0)
 
     @pl.when(c == 1)
     def _():
         decodes()
 
-    scatter1(3)
-    scatter2(1)
+    scatter1(0)
+    scatter1(1)
 
     def second_step(s, carry):
-        @pl.when(s < NN)
-        def _():
-            scatter0(1, s)
-
-        @pl.when(s < 2)
-        def _():
-            scatter2(s + 2)
-
-        @pl.when((s >= 2) & (s < 6))
-        def _():
-            scatter1(s + 2)
-
-        @pl.when((s >= 4) & (s < 8))
-        def _():
-            scatter2(s)
-
-        @pl.when(s < 4)
-        def _():
-            scatter3(0, s)
-            written(0, s).start()
+        @pl.when(s < NC)
+        def _():
+            scatter0(1, s - NN)
+
+        @pl.when(s < NC + 2)
+        def _():
+            scatter1(s - 2)
+
+        @pl.when(s < NC + 4)
+        def _():
+            scatter2(s - 4)
 
         @pl.when(s >= 6)
         def _():
-            scatter3(1, s - 6)
-            written(1, s - 6).start()
+            i = s - 6
+            scatter3(i // NN, i % NN)
+            written(i // NN, i % NN).start()
 
         return carry
 
-    lax.fori_loop(0, 10, second_step, 0)
+    lax.fori_loop(NN, NC + 6, second_step, 0)
 
     def drain(i, carry):
         for k in range(17):

time: 81.8 us -> 80.6 us (0.985)
  Pallas kernels: 79.8 us -> 78.1 us
    pallas_call x1, Pallas kernels: 79.8 us -> 78.1 us  [shards(): pl.pallas_call(kernel, name='block', out_shape=jax.ShapeDtypeStruct((32,...]
where the time goes in v5:
time: 80.6 us; the launch traced here: 80 us
  Pallas kernels  78.1 us (97%)
  local copies, waits for them, and re-layouts  1.87 us (2%)
    pallas_call x1, Pallas kernels, shards(): pl.pallas_call(kernel, name='block', out_shape=jax.ShapeDtypeStruct((32,...  78.1 us
    unnamed x1, local copies, waits for them, and re-layouts  1.87 us

profile of v5, /device:TPU:160, one launch (start us, length us, event | category | flops | bytes accessed | tf_op | source)
XLA Modules:
  0.0 80.0 jit_solution(4928573804406322998)
XLA Ops:
  0.0 78.1 %block.1 = bf16[32,8192]{1,0:T(8,128)(2,1)} custom-call(bf16[32,8192]{1,0:T(8,128)(2,1)} %x_hbm.1, f32[1,8192]{1,0:T(1,128)} %bitcast.2, f32[1,128]{1,0:T(1,128)} %constant.7.freq_hbm, bf16[8192,256]{1,0:T(8,128)(2,1)} %wq_hbm.1, bf16[8192,128]{1,0:T(8,128)(2,1)} %wkv_hbm.1, bf16[256,8192]{1,0:T(8,128)(2,1)} %wo_hbm.1, bf16[8,128,256]{2,1,0:T(8,128)(2,1)} %pool_hbm.1, ...), custom_call_target="tpu_custom_call" | custom-call | tf_op jit(solution)/shard_map/block/pallas_call | solution.py:550
  78.1 1.9 %copy.12 = bf16[32,8192]{1,0:T(8,128)(2,1)} copy(bf16[32,8192]{1,0:T(8,128)(2,1)} %block.1) | data formatting | bytes 1048576

commit v6 on v5

--- a/solution.py
+++ b/solution.py
@@ -314,7 +314,7 @@
             pc[rows, :] = e.astype(BF16)
             return carry
 
-        lax.fori_loop(0, n // 32, some, 0, unroll=2)
+        lax.fori_loop(0, n // 32, some, 0, unroll=True)
         o_ref[b, st, 0:n, :] = jnp.dot(pc[0:n, :], kvc[st, :, HD : 2 * HD], preferred_element_type=F32)
 
     def fresh(b, st):

time: 80.6 us -> 79.8 us (0.990)
  no operation moved by 1% of the time
where the time goes in v6:
time: 79.8 us; the launch traced here: 79.7 us
  Pallas kernels  77.8 us (97%)
  local copies, waits for them, and re-layouts  1.87 us (2%)
    pallas_call x1, Pallas kernels, shards(): pl.pallas_call(kernel, name='block', out_shape=jax.ShapeDtypeStruct((32,...  77.8 us
    unnamed x1, local copies, waits for them, and re-layouts  1.87 us

profile of v6, /device:TPU:160, one launch (start us, length us, event | category | flops | bytes accessed | tf_op | source)
XLA Modules:
  0.0 79.7 jit_solution(10862893006091130722)
XLA Ops:
  0.0 77.8 %block.1 = bf16[32,8192]{1,0:T(8,128)(2,1)} custom-call(bf16[32,8192]{1,0:T(8,128)(2,1)} %x_hbm.1, f32[1,8192]{1,0:T(1,128)} %bitcast.2, f32[1,128]{1,0:T(1,128)} %constant.7.freq_hbm, bf16[8192,256]{1,0:T(8,128)(2,1)} %wq_hbm.1, bf16[8192,128]{1,0:T(8,128)(2,1)} %wkv_hbm.1, bf16[256,8192]{1,0:T(8,128)(2,1)} %wo_hbm.1, bf16[8,128,256]{2,1,0:T(8,128)(2,1)} %pool_hbm.1, ...), custom_call_target="tpu_custom_call" | custom-call | tf_op jit(solution)/shard_map/block/pallas_call | solution.py:550
  77.8 1.9 %copy.12 = bf16[32,8192]{1,0:T(8,128)(2,1)} copy(bf16[32,8192]{1,0:T(8,128)(2,1)} %block.1) | data formatting | bytes 1048576

commit v7 on v6

--- a/solution.py
+++ b/solution.py
@@ -370,7 +370,7 @@
                 o = o + jnp.dot(
                     pd[rows, b * 128 : (b + 1) * 128], pool[b, :, HD : 2 * HD], preferred_element_type=F32
                 )
-            att[1, 112:128, n * HD : (n + 1) * HD] = (o / tot).astype(BF16)
+            sd[rows, 0:HD] = o / tot
 
     lax.fori_loop(0, NC + 1, gather_step, 0)
     gather1(7)
@@ -395,6 +395,11 @@
     exchange(1)
     project(1, 3, 256, 512)
     place_queries(1)
+
+    @pl.when(c == 1)
+    def _():
+        decodes()
+
     for b in range(NB):
         swap_new(b, 0).wait_recv()
         swap_new(b, 1).wait_recv()
@@ -493,7 +498,8 @@
 
     @pl.when(c == 1)
     def _():
-        decodes()
+        for n in range(4):
+            att[1, 112:128, n * HD : (n + 1) * HD] = sd[n * 16 : (n + 1) * 16, 0:HD].astype(BF16)
 
     scatter1(0)
     scatter1(1)

time: 79.8 us -> 79.7 us (level)
  no operation moved by 1% of the time
where the time goes in v7:
time: 79.7 us; the launch traced here: 79.5 us
  Pallas kernels  77.7 us (97%)
  local copies, waits for them, and re-layouts  1.87 us (2%)
    pallas_call x1, Pallas kernels, shards(): pl.pallas_call(kernel, name='block', out_shape=jax.ShapeDtypeStruct((32,...  77.7 us
    unnamed x1, local copies, waits for them, and re-layouts  1.87 us

profile of v7, /device:TPU:160, one launch (start us, length us, event | category | flops | bytes accessed | tf_op | source)
XLA Modules:
  0.0 79.5 jit_solution(9145901293601134024)
XLA Ops:
  0.0 77.7 %block.1 = bf16[32,8192]{1,0:T(8,128)(2,1)} custom-call(bf16[32,8192]{1,0:T(8,128)(2,1)} %x_hbm.1, f32[1,8192]{1,0:T(1,128)} %bitcast.2, f32[1,128]{1,0:T(1,128)} %constant.7.freq_hbm, bf16[8192,256]{1,0:T(8,128)(2,1)} %wq_hbm.1, bf16[8192,128]{1,0:T(8,128)(2,1)} %wkv_hbm.1, bf16[256,8192]{1,0:T(8,128)(2,1)} %wo_hbm.1, bf16[8,128,256]{2,1,0:T(8,128)(2,1)} %pool_hbm.1, ...), custom_call_target="tpu_custom_call" | custom-call | tf_op jit(solution)/shard_map/block/pallas_call | solution.py:556
  77.7 1.9 %copy.12 = bf16[32,8192]{1,0:T(8,128)(2,1)} copy(bf16[32,8192]{1,0:T(8,128)(2,1)} %block.1) | data formatting | bytes 1048576
